TPU v7x, 512 devices: a whole 4x8x8 slice. The times are simulated.
512 devices in a mesh: blk: 128 (over z, y, core), dir: 4 (over x).
Axes of the slice: x: 4, y: 8, z: 8, core: 2. Of those that a mesh axis runs over, the one named last changes fastest.
Arguments:
- spectrum: float32 [36, 36, 2048, 128], P('dir', None, 'blk'), may hold values from 0 to 4.5, as said below
- group_speed: float32 [36, 2048, 128], P(None, 'blk'), may hold values from 0.3 to 1
- ocean_current: float32 [2, 128, 2048], P(None, 'blk'), may hold values from -0.5 to 0.5
- route_slot: int32 [2048, 128], P('blk'), may hold values from -1 to 2047, as said below
- wind_vector: float32 [128, 2, 2048], P('blk'), may hold values from -4 to 4
- ice_cover: float32 [128, 2048], P('blk'), may hold values from 0 to 0.9
Outputs:
- spectrum_out: float32 [36, 36, 2048, 128], P('dir', None, 'blk')
- ocean_forcing: float32 [4, 128, 2048], P('dir', 'blk')
Inputs may be any that keep to these rules, and one draw needn't show every extreme that they name: `route_slot`: on one geographic block the sea cells routed to one owner use slots 0 to their count - 1, at most 16 of them; some owner receives 16 cells from every block. Land cells hold -1. `spectrum`: positive everywhere.
All inputs are finite; a program needn't handle non-finite values.
Results may differ from a plain program's by a relative error of at most 0.00002.
Values sent between devices are 32-bit elements; how exact they have to be, the bound alone decides.
No kernel may reach another device: no remote copies, remote signals or barrier semaphores. Data moves between devices by JAX's collectives and lax.ppermute only.
A program may use at most 64 MiB of HBM per device.

v0:
```python
import jax
import jax.numpy as jnp
import numpy as np
from jax import lax
from jax.experimental import pallas as pl
from jax.experimental.pallas import tpu as pltpu
from jax.sharding import PartitionSpec as P


BLK = "blk"
DIR = "dir"
VMEM = pltpu.VMEM
SMEM = pltpu.SMEM

COURANT = 0.15
WIND_GROWTH = 0.15
DAMP_RATE = 0.5
STEEP_COEF = 0.01
STOKES_SCALE = 0.15
RATIO_STEP = 1.1

LANES = 128
BANDS = 4
MIB = 1 << 20
UNROLL = 18
ROWS = 16
CUR_X, CUR_Y, WIND_X, WIND_Y, ICE = 0, 24, 48, 64, 80


def vmem_specs(count):
    return [pl.BlockSpec(memory_space=VMEM)] * count


def lane_of(shape):
    return lax.broadcasted_iota(jnp.int32, shape, len(shape) - 1)


def outgoing_kernel(
    bins,
    freqs,
    at_ref,
    cur_hbm,
    wind_hbm,
    ice_hbm,
    spec_hbm,
    speed_hbm,
    slot_hbm,
    out_ref,
    pair_ref,
    next_ref,
    cur_ref,
    wind_ref,
    ice_ref,
    spec_ref,
    speed_ref,
    slot_ref,
    x_ref,
    sems,
):
    sources = (cur_hbm, wind_hbm, ice_hbm, slot_hbm, speed_hbm, spec_hbm)
    targets = (cur_ref, wind_ref, ice_ref, slot_ref, speed_ref, spec_ref)
    copies = [pltpu.make_async_copy(a, b, sems.at[i]) for i, (a, b) in enumerate(zip(sources, targets))]
    for copy in copies:
        copy.start()
    for copy in copies[:3]:
        copy.wait()
    for c in range(2):
        for r in range(ROWS):
            x_ref[c, r : r + 1, :] = wind_ref[c : c + 1, LANES * r : LANES * (r + 1)]
    lane = lane_of((ROWS, LANES))

    def put(s, values, start):
        return pltpu.roll(values, (start - ROWS * s) % LANES, 1)

    for s in range(8):
        row = jnp.where(lane < CUR_Y, put(s, cur_ref[0], CUR_X + 1), put(s, cur_ref[1], CUR_Y))
        row = jnp.where(lane < WIND_X, row, put(s, x_ref[0], WIND_X))
        row = jnp.where(lane < WIND_Y, row, put(s, x_ref[1], WIND_Y))
        row = jnp.where(lane < ICE, row, put(s, ice_ref[...], ICE))
        out_ref[pl.ds(s, ROWS, stride=8), :] = row
    whole = out_ref[...]
    wide = lane_of((LANES, LANES))
    before = pltpu.roll(pltpu.roll(whole, 1, 0), LANES - ROWS, 1)
    after = pltpu.roll(pltpu.roll(whole, LANES - 1, 0), ROWS, 1)
    whole = jnp.where(wide == CUR_X, before, whole)
    out_ref[...] = jnp.where(wide == CUR_X + ROWS + 1, after, whole)
    odd = at_ref[0] >= BANDS
    for copy in copies[3:]:
        copy.wait()

    def trade(start, stop, first, last):
        pair_ref[start:stop, :] = jnp.where(odd, first, last)
        next_ref[start:stop, :] = jnp.where(odd, last, first)

    for source, start, count in ((spec_ref, 0, bins), (speed_ref, bins, freqs)):
        trade(start, start + count, source[pl.ds(0, count, stride=ROWS), :], source[pl.ds(ROWS - 1, count, stride=ROWS), :])
    sea = jnp.where(slot_ref[...] >= 0, 1.0, 0.0)
    sea = [jnp.broadcast_to(sea[r : r + 1, :], (8, LANES)) for r in (0, ROWS - 1)]
    trade(bins + freqs, bins + freqs + 8, *sea)


def move_kernel(
    dirs,
    freqs,
    at_ref,
    trig_ref,
    got_ref,
    spec_ref,
    speed_ref,
    pair_ref,
    next_ref,
    slot_ref,
    stored_ref,
    parts_ref,
    cell_ref,
    turned_ref,
    sx_ref,
    sy_ref,
    sw_ref,
    s16_ref,
    f16_ref,
    moved_ref,
    low_ref,
    high_ref,
    sems,
):
    shape = (ROWS, LANES)
    row, lane = lax.broadcasted_iota(jnp.int32, shape, 0), lane_of(shape)
    bins = dirs * freqs
    turned_ref[...] = got_ref[...].T
    odd = at_ref[0] >= BANDS
    low_ref[...] = jnp.where(odd, pair_ref[...], next_ref[...])
    high_ref[...] = jnp.where(odd, next_ref[...], pair_ref[...])

    def shifted_down(values, first):
        return jnp.where(row == 0, jnp.broadcast_to(first, shape), pltpu.roll(values, 1, 0))

    def next_y(values):
        return pltpu.roll(values, LANES - 1, 1)

    slots = slot_ref[...]
    sea = jnp.where(slots >= 0, 1.0, 0.0)
    sea_low, sea_high = low_ref[bins + freqs : bins + freqs + 1, :], high_ref[bins + freqs : bins + freqs + 1, :]
    half = 0.5 * COURANT
    open_x = half * sea * shifted_down(sea, sea_low)
    open_y = jnp.where(lane < LANES - 1, half * sea * next_y(sea), 0.0)
    open_16 = half * sea[ROWS - 1 : ROWS, :] * sea_high
    flow_x = open_x * (turned_ref[CUR_X : CUR_X + ROWS, :] + turned_ref[CUR_X + 1 : CUR_X + ROWS + 1, :])
    flow_16 = open_16 * (turned_ref[CUR_X + ROWS : CUR_X + ROWS + 1, :] + turned_ref[CUR_X + ROWS + 1 : CUR_X + ROWS + 2, :])
    cur_y = turned_ref[CUR_Y : CUR_Y + ROWS, :]
    flow_y = open_y * (cur_y + next_y(cur_y))
    flow_w = pltpu.roll(flow_y, 1, 1)

    owner, place = jnp.maximum(slots, 0) // 16, jnp.where(slots >= 0, slots % 16, -1)
    wind_x, wind_y, ice = (jnp.zeros(shape, jnp.float32) for _ in range(3))
    for s in range(16):
        here = place == s

        def picked(start, old):
            table = jnp.broadcast_to(turned_ref[start + s : start + s + 1, :], shape)
            return jnp.where(here, jnp.take_along_axis(table, owner, axis=1), old)

        wind_x, wind_y, ice = picked(WIND_X, wind_x), picked(WIND_Y, wind_y), picked(ICE, ice)
    gain = WIND_GROWTH * (1.0 - ice)
    cell_ref[0:16, :] = wind_x
    cell_ref[16:32, :] = wind_y
    cell_ref[32:48, :] = gain

    def faces(k, _):
        base = pl.multiple_of(k * ROWS, ROWS)
        speed = speed_ref[pl.ds(base, ROWS), :]
        sx_ref[pl.ds(base, ROWS), :] = open_x * (speed + shifted_down(speed, low_ref[pl.ds(bins + k, 1), :]))
        side = open_y * (speed + next_y(speed))
        sy_ref[pl.ds(base, ROWS), :] = side
        sw_ref[pl.ds(base, ROWS), :] = pltpu.roll(side, 1, 1)
        return 0

    lax.fori_loop(0, freqs, faces, 0, unroll=12)
    s16_ref[...] = open_16 * (speed_ref[pl.ds(ROWS - 1, freqs, stride=ROWS), :] + high_ref[bins : bins + freqs, :])

    zero = jnp.zeros(shape, jnp.float32)
    moment, stress_x, stress_y, drift_x, drift_y, damp_x, damp_y = (zero,) * 7
    at = at_ref[0] % BANDS
    copies = []
    for j in range(dirs):
        cosine, sine = trig_ref[at, j], trig_ref[at, dirs + j]
        face = s16_ref[...] * cosine + flow_16
        f16_ref[...] = face * jnp.where(
            face > 0.0,
            spec_ref[pl.ds(j * freqs * ROWS + ROWS - 1, freqs, stride=ROWS), :],
            high_ref[j * freqs : (j + 1) * freqs, :],
        )

        def step(k, sums):
            second, third, fourth = sums
            base = pl.multiple_of(k * ROWS, ROWS)
            here = pl.multiple_of(j * freqs * ROWS + k * ROWS, ROWS)
            energy = spec_ref[pl.ds(here, ROWS), :]
            u = sx_ref[pl.ds(base, ROWS), :] * cosine + flow_x
            below = u * jnp.where(u > 0.0, shifted_down(energy, low_ref[pl.ds(j * freqs + k, 1), :]), energy)
            above = jnp.where(
                row == ROWS - 1, jnp.broadcast_to(f16_ref[pl.ds(k, 1), :], shape), pltpu.roll(below, ROWS - 1, 0)
            )
            v = sy_ref[pl.ds(base, ROWS), :] * sine + flow_y
            right = v * jnp.where(v > 0.0, energy, next_y(energy))
            w = sw_ref[pl.ds(base, ROWS), :] * sine + flow_w
            left = w * jnp.where(w > 0.0, pltpu.roll(energy, 1, 1), energy)
            moved = sea * (energy - ((above - below) + (right - left)))
            moved_ref[pl.ds(here, ROWS), :] = moved
            return (
                second * (RATIO_STEP**-2) + moved,
                third * (RATIO_STEP**-3) + moved,
                fourth * (RATIO_STEP**-4) + moved,
            )

        def out_copy():
            part = pl.ds(j * freqs * ROWS, freqs * ROWS)
            return pltpu.make_async_copy(moved_ref.at[part, :], stored_ref.at[part, :], sems.at[j])

        second, third, fourth = lax.fori_loop(0, freqs, step, (zero, zero, zero), unroll=UNROLL)
        copies.append(out_copy())
        copies[-1].start()
        wind_gain = gain * jnp.maximum(wind_x * cosine + wind_y * sine, 0.0)
        push = wind_gain * second
        drift = third + wind_gain * fourth
        moment += second
        stress_x += cosine * push
        stress_y += sine * push
        drift_x += cosine * drift
        drift_y += sine * drift
        damp_x += cosine * fourth
        damp_y += sine * fourth
    for c, (main, damped) in enumerate(((stress_x, zero), (stress_y, zero), (drift_x, damp_x), (drift_y, damp_y))):
        parts_ref[c, 0:16, :] = moment
        parts_ref[c, 16:32, :] = main
        parts_ref[c, 32:48, :] = damped
    for copy in copies:
        copy.wait()


def forcing_kernel(at_ref, parts_ref, damping_ref, out_ref):
    parts = (parts_ref[0] + parts_ref[1]) + (parts_ref[2] + parts_ref[3])
    steepness = STEEP_COEF * parts[0:16]
    damping = DAMP_RATE * steepness / (1.0 + steepness)
    damping_ref[...] = damping
    own = parts[16:32] - damping * parts[32:48]
    own = jnp.where(at_ref[0] % BANDS < 2, 1.0, STOKES_SCALE) * own
    out_ref[...] = jnp.concatenate([own, jnp.zeros((LANES - ROWS, LANES), jnp.float32)], axis=0).T


def update_kernel(dirs, freqs, at_ref, trig_ref, moved_ref, cell_ref, damping_ref, out_ref):
    j, at = pl.program_id(0), at_ref[0] % BANDS
    cosine, sine = trig_ref[at, j], trig_ref[at, dirs + j]
    wind = jnp.maximum(cell_ref[0:16, :] * cosine + cell_ref[16:32, :] * sine, 0.0)
    growth = cell_ref[32:48, :] * wind - damping_ref[...]
    for k in range(freqs):
        ratio = RATIO_STEP ** (k - freqs + 1)
        out_ref[k * ROWS : (k + 1) * ROWS, :] = moved_ref[k * ROWS : (k + 1) * ROWS, :] * (1.0 + ratio * growth)


def row_kernel(got_ref, out_ref):
    lane = lane_of((ROWS, LANES))
    row = got_ref[pl.ds(0, ROWS, stride=8), :]
    for s in range(1, 8):
        row = jnp.where(lane < ROWS * s, row, pltpu.roll(got_ref[pl.ds(s, ROWS, stride=8), :], ROWS * s, 1))
    out_ref[...] = row


def f32(*shape):
    return jax.ShapeDtypeStruct(shape, jnp.float32)


def near(*shape):
    return VMEM(shape, jnp.float32)


def held(value):
    return pltpu.with_memory_space_constraint(value, VMEM)


def one_step(spectrum, group_speed, ocean_current, route_slot, wind_vector, ice_cover):
    dirs, freqs, _, _ = spectrum.shape
    bands, blocks = lax.axis_size(DIR), lax.axis_size(BLK)
    bins = dirs * freqs
    at = (lax.axis_index(DIR) + bands * (lax.axis_index(BLK) & 1)).astype(jnp.int32).reshape(1)
    angles = (2.0 * np.pi * np.arange(bands * dirs, dtype=np.float32) / np.float32(bands * dirs)).astype(np.float32)
    angles = angles.astype(np.float64).reshape(bands, dirs)
    trig = jnp.asarray(np.concatenate([np.cos(angles), np.sin(angles)], axis=1).astype(np.float32))
    smem = pl.BlockSpec(memory_space=SMEM)

    def far(value):
        return pltpu.with_memory_space_constraint(value, pltpu.HBM)

    flat = spectrum.reshape(bins * ROWS, LANES)
    speed = group_speed.reshape(freqs * ROWS, LANES)
    edge = pltpu.HBM((bins + freqs + 8, LANES), jnp.float32)
    messages, to_pair, to_next = pl.pallas_call(
        lambda *refs: outgoing_kernel(bins, freqs, *refs),
        out_shape=(near(LANES, LANES), edge, edge),
        in_specs=[smem] + [pl.BlockSpec(memory_space=pltpu.HBM)] * 6,
        out_specs=tuple(vmem_specs(3)),
        scratch_shapes=[
            VMEM((2, ROWS, LANES), jnp.float32),
            VMEM((2, ROWS * LANES), jnp.float32),
            VMEM((ROWS, LANES), jnp.float32),
            VMEM((bins * ROWS, LANES), jnp.float32),
            VMEM((freqs * ROWS, LANES), jnp.float32),
            VMEM((ROWS, LANES), jnp.int32),
            VMEM((2, ROWS, LANES), jnp.float32),
            pltpu.SemaphoreType.DMA((6,)),
        ],
        name="outgoing",
        compiler_params=pltpu.CompilerParams(vmem_limit_bytes=8 * MIB),
    )(
        at,
        far(ocean_current.reshape(2, ROWS, LANES)),
        far(wind_vector.reshape(2, ROWS * LANES)),
        far(ice_cover.reshape(ROWS, LANES)),
        far(flat),
        far(speed),
        far(route_slot),
    )
    pairs = [(i, i + 1) for i in range(0, blocks, 2)]
    nexts = [(i, i + 1) for i in range(1, blocks - 1, 2)]
    got = held(lax.all_to_all(messages, BLK, 0, 0, tiled=True))
    from_next = held(lax.ppermute(to_next, BLK, nexts + [(j, i) for i, j in nexts]))
    from_pair = held(lax.ppermute(to_pair, BLK, pairs + [(j, i) for i, j in pairs]))
    flat, speed = held(flat), held(speed)

    moved, parts, cell = pl.pallas_call(
        lambda *refs: move_kernel(dirs, freqs, *refs),
        out_shape=(pltpu.HBM((bins * ROWS, LANES), jnp.float32), near(bands, 48, LANES), near(48, LANES)),
        in_specs=[smem, smem] + vmem_specs(6),
        out_specs=(pl.BlockSpec(memory_space=pltpu.HBM), *vmem_specs(2)),
        scratch_shapes=[
            VMEM((LANES, LANES), jnp.float32),
            VMEM((freqs * ROWS, LANES), jnp.float32),
            VMEM((freqs * ROWS, LANES), jnp.float32),
            VMEM((freqs * ROWS, LANES), jnp.float32),
            VMEM((freqs, LANES), jnp.float32),
            VMEM((freqs, LANES), jnp.float32),
            VMEM((bins * ROWS, LANES), jnp.float32),
            VMEM((bins + freqs + 8, LANES), jnp.float32),
            VMEM((bins + freqs + 8, LANES), jnp.float32),
            pltpu.SemaphoreType.DMA((dirs,)),
        ],
        name="move",
        compiler_params=pltpu.CompilerParams(vmem_limit_bytes=8 * MIB),
    )(at, trig, got, flat, speed, from_pair, from_next, route_slot)

    parts = held(lax.all_to_all(parts, DIR, 0, 0, tiled=True))
    damping, own = pl.pallas_call(
        forcing_kernel,
        out_shape=(near(ROWS, LANES), near(LANES, LANES)),
        in_specs=[smem] + vmem_specs(1),
        out_specs=tuple(vmem_specs(2)),
        name="forcing",
        compiler_params=pltpu.CompilerParams(vmem_limit_bytes=4 * MIB),
    )(at, parts)
    ocean = held(lax.all_to_all(own, BLK, 0, 0, tiled=True))
    result = pl.pallas_call(
        lambda *refs: update_kernel(dirs, freqs, *refs),
        out_shape=f32(bins * ROWS, LANES),
        grid=(dirs,),
        in_specs=[smem, smem, pl.BlockSpec((freqs * ROWS, LANES), lambda j: (j, 0))] + vmem_specs(2),
        out_specs=pl.BlockSpec((freqs * ROWS, LANES), lambda j: (j, 0)),
        name="update",
        compiler_params=pltpu.CompilerParams(vmem_limit_bytes=4 * MIB),
        cost_estimate=pl.CostEstimate(flops=3 * bins * ROWS * LANES, bytes_accessed=8 * bins * ROWS * LANES, transcendentals=0),
    )(at, trig, pltpu.with_memory_space_constraint(moved, pltpu.HBM), cell, damping)
    ocean = pl.pallas_call(
        row_kernel,
        out_shape=f32(ROWS, LANES),
        in_specs=vmem_specs(1),
        out_specs=vmem_specs(1)[0],
        name="rows",
        compiler_params=pltpu.CompilerParams(vmem_limit_bytes=4 * MIB),
    )(ocean)
    return (result.reshape(spectrum.shape), ocean.reshape(1, 1, ROWS * LANES))


def solution(mesh):
    return jax.shard_map(
        one_step,
        mesh=mesh,
        in_specs=(
            P(DIR, None, BLK, None),
            P(None, BLK, None),
            P(None, BLK, None),
            P(BLK, None),
            P(BLK, None, None),
            P(BLK, None),
        ),
        out_specs=(P(DIR, None, BLK, None), P(DIR, BLK, None)),
        check_vma=False,
    )
```

profile of v0, /device:TPU:1, one launch (start us, length us, event | category | flops | bytes accessed | tf_op | source)
XLA Modules:
  0.0 71.8 jit_solution(396597766398908823)
XLA Ops:
  0.6 0.0 copy-start.3
  0.6 0.0 copy-start.2
  0.7 0.0 copy-start.1
  0.7 0.0 copy-start
  0.7 3.0 %outgoing.1 = (f32[128,128]{1,0:T(8,128)S(1)}, f32[368,128]{1,0:T(8,128)}, f32[368,128]{1,0:T(8,128)}) custom-call(s32[1]{0:T(128)} %bitcast.refs_0_.at_ref, f32[2,16,128]{2,1,0:T(8,128)} %bitcast.24, f32[2,2048]{1,0:T(2,128)} %bitcast.25, f32[16,128]{1,0:T(8,128)} %bitcast.26, f32[5184,128]{1,0:T(8,128)} %bitcast.16, f32[576,128]{1,0:T(8,128)} %bitcast.18, ...), custom_call_target="tpu_custom_call" | custom-call | tf_op jit(solution)/shard_map/outgoing/pallas_call | solution.py:297
  3.6 8.7 %collective-permute-start = (f32[368,128]{1,0:T(8,128)}, f32[368,128]{1,0:T(8,128)S(1)}, u32[]{:S(2)}, u32[]{:S(2)}) collective-permute-start(f32[368,128]{1,0:T(8,128)} %get-tuple-element.11), channel_id=1, source_target_pairs={{0,4},{8,12},{16,20},{24,28},{32,36},{40,44},{48,52},{56,60},{64,6... | collective-permute-start | bytes 565256 | tf_op jit(solution)/shard_map/ppermute | solution.py:327
  12.4 1.9 %collective-permute-start.1 = (f32[368,128]{1,0:T(8,128)}, f32[368,128]{1,0:T(8,128)S(1)}, u32[]{:S(2)}, u32[]{:S(2)}) collective-permute-start(f32[368,128]{1,0:T(8,128)} %get-tuple-element.12), channel_id=1, source_target_pairs={{4,8},{12,16},{20,24},{28,32},{36,40},{44,48},{52,56},{60,64},{68,... | collective-permute-start | bytes 565256 | tf_op jit(solution)/shard_map/ppermute | solution.py:326
  14.3 23.5 %all_to_all.27 = f32[128,1,128]{2,1,0:T(1,128)S(1)} all-to-all(f32[128,1,128]{2,1,0:T(1,128)S(1)} %bitcast.22), channel_id=1, replica_groups=mesh['blk'=128,'dir'=4] {'blk'}, dimensions={0} | all-to-all | bytes 131072 | tf_op jit(solution)/shard_map/all_to_all | solution.py:325
  37.9 0.0 collective-permute-done.refs_5_
  37.9 0.0 collective-permute-done.1.refs_6_
  37.9 0.0 copy-done.3
  37.9 0.0 copy-done.2
  37.9 0.0 copy-done.1
  37.9 0.0 copy-done
  37.9 5.4 %move.1 = (f32[5184,128]{1,0:T(8,128)}, f32[4,48,128]{2,1,0:T(8,128)S(1)}, f32[48,128]{1,0:T(8,128)S(1)}) custom-call(s32[1]{0:T(128)} %bitcast.refs_0_.at_ref, f32[4,18]{1,0:T(4,128)S(1)} %copy-done.3, f32[128,128]{1,0:T(8,128)S(1)} %bitcast.20, f32[5184,128]{1,0:T(8,128)S(1)} %bitcast.17, f32[576,128]{1,0:T(8,128)S(1)} %bitcast.19, ...), custom_call_target="tpu_custom_call" | custom-call | tf_op jit(solution)/shard_map/move/pallas_call | solution.py:330
  43.3 8.5 %all_to_all.28.parts_ref = f32[4,48,128]{2,1,0:T(8,128)S(1)} all-to-all(f32[4,48,128]{2,1,0:T(8,128)S(1)} %get-tuple-element.15), channel_id=1, replica_groups=mesh['blk'=128,'dir'=4] {'dir'}, dimensions={0} | all-to-all | bytes 196608 | tf_op jit(solution)/shard_map/all_to_all | solution.py:351
  51.8 0.7 %forcing.1 = (f32[16,128]{1,0:T(8,128)S(1)}, f32[128,128]{1,0:T(8,128)}) custom-call(s32[1]{0:T(128)} %bitcast.refs_0_.at_ref, f32[4,48,128]{2,1,0:T(8,128)S(1)} %all_to_all.28.parts_ref), custom_call_target="tpu_custom_call" | custom-call | tf_op jit(solution)/shard_map/forcing/pallas_call | solution.py:352
  52.5 7.1 %all-to-all-start.2 = ((f32[128,1,128]{2,1,0:T(1,128)}), f32[128,1,128]{2,1,0:T(1,128)S(1)}, u32[]{:S(2)}, u32[]{:S(2)}) async-start(f32[128,1,128]{2,1,0:T(1,128)} %bitcast.11), calls=%async_computation.2 | async-start | bytes 131072 | tf_op jit(solution)/shard_map/all_to_all | solution.py:360
  59.6 6.5 %update.1 = f32[5184,128]{1,0:T(8,128)} custom-call(s32[1]{0:T(128)} %bitcast.refs_0_.at_ref, f32[4,18]{1,0:T(4,128)S(1)} %copy-done.3, f32[5184,128]{1,0:T(8,128)} %get-tuple-element.13.refs_2_, f32[48,128]{1,0:T(8,128)S(1)} %get-tuple-element.14.refs_3_, f32[16,128]{1,0:T(8,128)S(1)} %get-tuple-element.16.refs_4_), custom_call_target="tpu_custom_call" | custom-call | flops 1990656 | bytes 5308416 | tf_op jit(solution)/shard_map/update/pallas_call | solution.py:361
  66.1 5.0 %all-to-all-done.2 = f32[128,1,128]{2,1,0:T(1,128)S(1)} async-done(((f32[128,1,128]{2,1,0:T(1,128)}), f32[128,1,128]{2,1,0:T(1,128)S(1)}, u32[]{:S(2)}, u32[]{:S(2)}) %all-to-all-start.2) | async-done | bytes 65568 | tf_op jit(solution)/shard_map/all_to_all | solution.py:360
  71.2 0.7 rows.1
Async XLA Ops:
  0.6 37.2 %copy-start.3 = (f32[4,18]{1,0:T(4,128)S(1)}, f32[4,18]{1,0:T(4,128)}, u32[]{:S(2)}) copy-start(f32[4,18]{1,0:T(4,128)} %constant.15.clone.refs_1_) | copy-start | bytes 868
  0.6 37.2 %copy-start.2 = (s32[16,128]{1,0:T(8,128)S(1)}, s32[16,128]{1,0:T(8,128)}, u32[]{:S(2)}) copy-start(s32[16,128]{1,0:T(8,128)} %refs_7_.1) | copy-start | bytes 24580
  0.7 37.2 %copy-start.1 = (f32[36,16,128]{2,1,0:T(8,128)S(1)}, f32[36,16,128]{2,1,0:T(8,128)}, u32[]{:S(2)}) copy-start(f32[36,16,128]{2,1,0:T(8,128)} %param.8) | copy-start | bytes 884740
  0.7 37.2 %copy-start = (f32[9,36,16,128]{3,2,1,0:T(8,128)S(1)}, f32[9,36,16,128]{3,2,1,0:T(8,128)}, u32[]{:S(2)}) copy-start(f32[9,36,16,128]{3,2,1,0:T(8,128)} %param.7) | copy-start | bytes 7962628
  3.6 34.2 %collective-permute-start = (f32[368,128]{1,0:T(8,128)}, f32[368,128]{1,0:T(8,128)S(1)}, u32[]{:S(2)}, u32[]{:S(2)}) collective-permute-start(f32[368,128]{1,0:T(8,128)} %get-tuple-element.11), channel_id=1, source_target_pairs={{0,4},{8,12},{16,20},{24,28},{32,36},{40,44},{48,52},{56,60},{64,6... | collective-permute-start | bytes 565256 | tf_op jit(solution)/shard_map/ppermute | solution.py:327
  12.4 25.5 %collective-permute-start.1 = (f32[368,128]{1,0:T(8,128)}, f32[368,128]{1,0:T(8,128)S(1)}, u32[]{:S(2)}, u32[]{:S(2)}) collective-permute-start(f32[368,128]{1,0:T(8,128)} %get-tuple-element.12), channel_id=1, source_target_pairs={{4,8},{12,16},{20,24},{28,32},{36,40},{44,48},{52,56},{60,64},{68,... | collective-permute-start | bytes 565256 | tf_op jit(solution)/shard_map/ppermute | solution.py:326
  52.5 18.6 %all-to-all-start.2 = ((f32[128,1,128]{2,1,0:T(1,128)}), f32[128,1,128]{2,1,0:T(1,128)S(1)}, u32[]{:S(2)}, u32[]{:S(2)}) async-start(f32[128,1,128]{2,1,0:T(1,128)} %bitcast.11), calls=%async_computation.2 | async-start | bytes 131072 | tf_op jit(solution)/shard_map/all_to_all | solution.py:360
where the time goes:
time: 72.2 us; the launch traced here: 71.8 us
  blocking collectives  32 us (44%)
  starting transfers between devices  17.7 us (25%)
  Pallas kernels  16.3 us (23%)
  waiting for transfers between devices  5.05 us (7%)
  between operations  0.74 us (1%)
    all_to_all x1, blocking collectives, one_step(): got = held(lax.all_to_all(messages, BLK, 0, 0, tiled=True))  23.5 us
    ppermute x1, starting transfers between devices, one_step(): lax.ppermute(to_pair, BLK, pairs + [(j, i) for i, j in pairs])  8.75 us
    all_to_all x1, blocking collectives, one_step(): parts = held(lax.all_to_all(parts, DIR, 0, 0, tiled=True))  8.47 us
    all_to_all x1, starting transfers between devices, one_step(): ocean = held(lax.all_to_all(own, BLK, 0, 0, tiled=True))  7.07 us
    pallas_call x1, Pallas kernels, one_step(): pl.pallas_call(lambda *refs: update_kernel(dirs, freqs, *refs), out_shape...  6.51 us
    pallas_call x1, Pallas kernels, one_step(): pl.pallas_call(lambda *refs: move_kernel(dirs, freqs, *refs), out_shape=(...  5.42 us
    all_to_all x1, waiting for transfers between devices, one_step(): ocean = held(lax.all_to_all(own, BLK, 0, 0, tiled=True))  5.05 us
    pallas_call x1, Pallas kernels, one_step(): pl.pallas_call(lambda *refs: outgoing_kernel(bins, freqs, *refs), out_sha...  2.95 us
  transfers between devices with their start and end apart: 3, of which 1 were waited for; matrix products, arithmetic and copies ran while one was open for 0% of the time, Pallas kernels for 9%

commit v1 on v0

--- a/solution.py
+++ b/solution.py
@@ -1,3 +1,5 @@
+import math
+
 import jax
 import jax.numpy as jnp
 import numpy as np
@@ -35,34 +37,22 @@
     return lax.broadcasted_iota(jnp.int32, shape, len(shape) - 1)
 
 
-def outgoing_kernel(
-    bins,
-    freqs,
-    at_ref,
+def message_kernel(
     cur_hbm,
     wind_hbm,
     ice_hbm,
-    spec_hbm,
-    speed_hbm,
-    slot_hbm,
     out_ref,
-    pair_ref,
-    next_ref,
     cur_ref,
     wind_ref,
     ice_ref,
-    spec_ref,
-    speed_ref,
-    slot_ref,
     x_ref,
     sems,
 ):
-    sources = (cur_hbm, wind_hbm, ice_hbm, slot_hbm, speed_hbm, spec_hbm)
-    targets = (cur_ref, wind_ref, ice_ref, slot_ref, speed_ref, spec_ref)
+    sources, targets = (cur_hbm, wind_hbm, ice_hbm), (cur_ref, wind_ref, ice_ref)
     copies = [pltpu.make_async_copy(a, b, sems.at[i]) for i, (a, b) in enumerate(zip(sources, targets))]
     for copy in copies:
         copy.start()
-    for copy in copies[:3]:
+    for copy in copies:
         copy.wait()
     for c in range(2):
         for r in range(ROWS):
@@ -84,9 +74,18 @@
     after = pltpu.roll(pltpu.roll(whole, LANES - 1, 0), ROWS, 1)
     whole = jnp.where(wide == CUR_X, before, whole)
     out_ref[...] = jnp.where(wide == CUR_X + ROWS + 1, after, whole)
+
+
+def edge_kernel(
+    bins, freqs, at_ref, spec_hbm, speed_hbm, slot_hbm, pair_ref, next_ref, spec_ref, speed_ref, slot_ref, sems
+):
+    sources, targets = (slot_hbm, speed_hbm, spec_hbm), (slot_ref, speed_ref, spec_ref)
+    copies = [pltpu.make_async_copy(a, b, sems.at[i]) for i, (a, b) in enumerate(zip(sources, targets))]
+    for copy in copies:
+        copy.start()
+    for copy in copies:
+        copy.wait()
     odd = at_ref[0] >= BANDS
-    for copy in copies[3:]:
-        copy.wait()
 
     def trade(start, stop, first, last):
         pair_ref[start:stop, :] = jnp.where(odd, first, last)
@@ -107,8 +106,6 @@
     got_ref,
     spec_ref,
     speed_ref,
-    pair_ref,
-    next_ref,
     slot_ref,
     stored_ref,
     parts_ref,
@@ -117,36 +114,25 @@
     sx_ref,
     sy_ref,
     sw_ref,
-    s16_ref,
-    f16_ref,
     moved_ref,
-    low_ref,
-    high_ref,
     sems,
 ):
     shape = (ROWS, LANES)
     row, lane = lax.broadcasted_iota(jnp.int32, shape, 0), lane_of(shape)
-    bins = dirs * freqs
     turned_ref[...] = got_ref[...].T
-    odd = at_ref[0] >= BANDS
-    low_ref[...] = jnp.where(odd, pair_ref[...], next_ref[...])
-    high_ref[...] = jnp.where(odd, next_ref[...], pair_ref[...])
-
-    def shifted_down(values, first):
-        return jnp.where(row == 0, jnp.broadcast_to(first, shape), pltpu.roll(values, 1, 0))
+
+    def shifted_down(values):
+        return pltpu.roll(values, 1, 0)
 
     def next_y(values):
         return pltpu.roll(values, LANES - 1, 1)
 
     slots = slot_ref[...]
     sea = jnp.where(slots >= 0, 1.0, 0.0)
-    sea_low, sea_high = low_ref[bins + freqs : bins + freqs + 1, :], high_ref[bins + freqs : bins + freqs + 1, :]
     half = 0.5 * COURANT
-    open_x = half * sea * shifted_down(sea, sea_low)
+    open_x = jnp.where(row > 0, half * sea * shifted_down(sea), 0.0)
     open_y = jnp.where(lane < LANES - 1, half * sea * next_y(sea), 0.0)
-    open_16 = half * sea[ROWS - 1 : ROWS, :] * sea_high
     flow_x = open_x * (turned_ref[CUR_X : CUR_X + ROWS, :] + turned_ref[CUR_X + 1 : CUR_X + ROWS + 1, :])
-    flow_16 = open_16 * (turned_ref[CUR_X + ROWS : CUR_X + ROWS + 1, :] + turned_ref[CUR_X + ROWS + 1 : CUR_X + ROWS + 2, :])
     cur_y = turned_ref[CUR_Y : CUR_Y + ROWS, :]
     flow_y = open_y * (cur_y + next_y(cur_y))
     flow_w = pltpu.roll(flow_y, 1, 1)
@@ -165,18 +151,19 @@
     cell_ref[0:16, :] = wind_x
     cell_ref[16:32, :] = wind_y
     cell_ref[32:48, :] = gain
+    for side, x in enumerate((CUR_X, CUR_X + ROWS)):
+        cell_ref[48 + side : 49 + side, :] = turned_ref[x : x + 1, :] + turned_ref[x + 1 : x + 2, :]
 
     def faces(k, _):
         base = pl.multiple_of(k * ROWS, ROWS)
         speed = speed_ref[pl.ds(base, ROWS), :]
-        sx_ref[pl.ds(base, ROWS), :] = open_x * (speed + shifted_down(speed, low_ref[pl.ds(bins + k, 1), :]))
+        sx_ref[pl.ds(base, ROWS), :] = open_x * (speed + shifted_down(speed))
         side = open_y * (speed + next_y(speed))
         sy_ref[pl.ds(base, ROWS), :] = side
         sw_ref[pl.ds(base, ROWS), :] = pltpu.roll(side, 1, 1)
         return 0
 
     lax.fori_loop(0, freqs, faces, 0, unroll=12)
-    s16_ref[...] = open_16 * (speed_ref[pl.ds(ROWS - 1, freqs, stride=ROWS), :] + high_ref[bins : bins + freqs, :])
 
     zero = jnp.zeros(shape, jnp.float32)
     moment, stress_x, stress_y, drift_x, drift_y, damp_x, damp_y = (zero,) * 7
@@ -184,12 +171,6 @@
     copies = []
     for j in range(dirs):
         cosine, sine = trig_ref[at, j], trig_ref[at, dirs + j]
-        face = s16_ref[...] * cosine + flow_16
-        f16_ref[...] = face * jnp.where(
-            face > 0.0,
-            spec_ref[pl.ds(j * freqs * ROWS + ROWS - 1, freqs, stride=ROWS), :],
-            high_ref[j * freqs : (j + 1) * freqs, :],
-        )
 
         def step(k, sums):
             second, third, fourth = sums
@@ -197,10 +178,8 @@
             here = pl.multiple_of(j * freqs * ROWS + k * ROWS, ROWS)
             energy = spec_ref[pl.ds(here, ROWS), :]
             u = sx_ref[pl.ds(base, ROWS), :] * cosine + flow_x
-            below = u * jnp.where(u > 0.0, shifted_down(energy, low_ref[pl.ds(j * freqs + k, 1), :]), energy)
-            above = jnp.where(
-                row == ROWS - 1, jnp.broadcast_to(f16_ref[pl.ds(k, 1), :], shape), pltpu.roll(below, ROWS - 1, 0)
-            )
+            below = u * jnp.where(u > 0.0, shifted_down(energy), energy)
+            above = pltpu.roll(below, ROWS - 1, 0)
             v = sy_ref[pl.ds(base, ROWS), :] * sine + flow_y
             right = v * jnp.where(v > 0.0, energy, next_y(energy))
             w = sw_ref[pl.ds(base, ROWS), :] * sine + flow_w
@@ -238,6 +217,64 @@
         copy.wait()
 
 
+def fix_kernel(
+    dirs,
+    freqs,
+    at_ref,
+    trig_ref,
+    cell_ref,
+    from_pair_ref,
+    from_next_ref,
+    to_pair_ref,
+    to_next_ref,
+    parts_ref,
+    out_ref,
+    fix_ref,
+    behind_ref,
+    ahead_ref,
+):
+    bins = dirs * freqs
+    odd, at = at_ref[0] >= BANDS, at_ref[0] % BANDS
+    power = lax.broadcasted_iota(jnp.int32, (freqs, LANES), 0).astype(jnp.float32) - (freqs - 1)
+    weights = [jnp.exp(power * (p * math.log(RATIO_STEP))) for p in (2, 3, 4)]
+    out_ref[...] = parts_ref[...]
+    faces = (
+        (0, 1.0, from_pair_ref, from_next_ref, to_pair_ref, to_next_ref),
+        (ROWS - 1, -1.0, to_next_ref, to_pair_ref, from_next_ref, from_pair_ref),
+    )
+    for side, (row, sign, behind_odd, behind_even, ahead_odd, ahead_even) in enumerate(faces):
+        behind_ref[...] = jnp.where(odd, behind_odd[...], behind_even[...])
+        ahead_ref[...] = jnp.where(odd, ahead_odd[...], ahead_even[...])
+        mask = slice(bins + freqs, bins + freqs + 1)
+        opened = (sign * 0.5 * COURANT) * behind_ref[mask, :] * ahead_ref[mask, :]
+        flow = opened * cell_ref[48 + side : 49 + side, :]
+        speed = opened * (behind_ref[bins : bins + freqs, :] + ahead_ref[bins : bins + freqs, :])
+        wind_x, wind_y, gain = (cell_ref[r : r + 1, :] for r in (row, 16 + row, 32 + row))
+        moment, stress_x, stress_y, drift_x, drift_y, damp_x, damp_y = (jnp.zeros((1, LANES), jnp.float32),) * 7
+        for j in range(dirs):
+            cosine, sine = trig_ref[at, j], trig_ref[at, dirs + j]
+            u = speed * cosine + flow
+            part = slice(j * freqs, (j + 1) * freqs)
+            flux = u * jnp.where(sign * u > 0.0, behind_ref[part, :], ahead_ref[part, :])
+            fix_ref[side, part, :] = flux
+            second, third, fourth = (jnp.sum(w * flux, axis=0, keepdims=True) for w in weights)
+            wind_gain = gain * jnp.maximum(wind_x * cosine + wind_y * sine, 0.0)
+            push = wind_gain * second
+            drift = third + wind_gain * fourth
+            moment += second
+            stress_x += cosine * push
+            stress_y += sine * push
+            drift_x += cosine * drift
+            drift_y += sine * drift
+            damp_x += cosine * fourth
+            damp_y += sine * fourth
+        for c, (main, damped) in enumerate(((stress_x, None), (stress_y, None), (drift_x, damp_x), (drift_y, damp_y))):
+            out_ref[c, row : row + 1, :] += moment
+            out_ref[c, 16 + row : 17 + row, :] += main
+            if damped is not None:
+                out_ref[c, 32 + row : 33 + row, :] += damped
+
+
 def forcing_kernel(at_ref, parts_ref, damping_ref, out_ref):
     parts = (parts_ref[0] + parts_ref[1]) + (parts_ref[2] + parts_ref[3])
     steepness = STEEP_COEF * parts[0:16]
@@ -248,14 +285,18 @@
     out_ref[...] = jnp.concatenate([own, jnp.zeros((LANES - ROWS, LANES), jnp.float32)], axis=0).T
 
 
-def update_kernel(dirs, freqs, at_ref, trig_ref, moved_ref, cell_ref, damping_ref, out_ref):
+def update_kernel(dirs, freqs, at_ref, trig_ref, moved_ref, cell_ref, damping_ref, fix_ref, out_ref):
     j, at = pl.program_id(0), at_ref[0] % BANDS
     cosine, sine = trig_ref[at, j], trig_ref[at, dirs + j]
     wind = jnp.maximum(cell_ref[0:16, :] * cosine + cell_ref[16:32, :] * sine, 0.0)
     growth = cell_ref[32:48, :] * wind - damping_ref[...]
+    row = lax.broadcasted_iota(jnp.int32, (ROWS, LANES), 0)
     for k in range(freqs):
         ratio = RATIO_STEP ** (k - freqs + 1)
-        out_ref[k * ROWS : (k + 1) * ROWS, :] = moved_ref[k * ROWS : (k + 1) * ROWS, :] * (1.0 + ratio * growth)
+        first, last = (jnp.broadcast_to(fix_ref[side, pl.ds(j * freqs + k, 1), :], (ROWS, LANES)) for side in (0, 1))
+        edge = jnp.where(row == 0, first, jnp.where(row == ROWS - 1, last, 0.0))
+        moved = moved_ref[k * ROWS : (k + 1) * ROWS, :] + edge
+        out_ref[k * ROWS : (k + 1) * ROWS, :] = moved * (1.0 + ratio * growth)
 
 
 def row_kernel(got_ref, out_ref):
@@ -291,62 +332,74 @@
     def far(value):
         return pltpu.with_memory_space_constraint(value, pltpu.HBM)
 
-    flat = spectrum.reshape(bins * ROWS, LANES)
-    speed = group_speed.reshape(freqs * ROWS, LANES)
-    edge = pltpu.HBM((bins + freqs + 8, LANES), jnp.float32)
-    messages, to_pair, to_next = pl.pallas_call(
-        lambda *refs: outgoing_kernel(bins, freqs, *refs),
-        out_shape=(near(LANES, LANES), edge, edge),
-        in_specs=[smem] + [pl.BlockSpec(memory_space=pltpu.HBM)] * 6,
-        out_specs=tuple(vmem_specs(3)),
+    messages = pl.pallas_call(
+        message_kernel,
+        out_shape=near(LANES, LANES),
+        in_specs=[pl.BlockSpec(memory_space=pltpu.HBM)] * 3,
+        out_specs=vmem_specs(1)[0],
         scratch_shapes=[
             VMEM((2, ROWS, LANES), jnp.float32),
             VMEM((2, ROWS * LANES), jnp.float32),
             VMEM((ROWS, LANES), jnp.float32),
+            VMEM((2, ROWS, LANES), jnp.float32),
+            pltpu.SemaphoreType.DMA((3,)),
+        ],
+        name="messages",
+        compiler_params=pltpu.CompilerParams(vmem_limit_bytes=4 * MIB),
+    )(
+        far(ocean_current.reshape(2, ROWS, LANES)),
+        far(wind_vector.reshape(2, ROWS * LANES)),
+        far(ice_cover.reshape(ROWS, LANES)),
+    )
+    flat, speed = spectrum.reshape(bins * ROWS, LANES), group_speed.reshape(freqs * ROWS, LANES)
+    edge = near(bins + freqs + 8, LANES)
+    edges = pl.pallas_call(
+        lambda *refs: edge_kernel(bins, freqs, *refs),
+        out_shape=(edge, edge),
+        in_specs=[smem] + [pl.BlockSpec(memory_space=pltpu.HBM)] * 3,
+        out_specs=tuple(vmem_specs(2)),
+        scratch_shapes=[
             VMEM((bins * ROWS, LANES), jnp.float32),
             VMEM((freqs * ROWS, LANES), jnp.float32),
             VMEM((ROWS, LANES), jnp.int32),
-            VMEM((2, ROWS, LANES), jnp.float32),
-            pltpu.SemaphoreType.DMA((6,)),
+            pltpu.SemaphoreType.DMA((3,)),
         ],
-        name="outgoing",
+        name="edges",
         compiler_params=pltpu.CompilerParams(vmem_limit_bytes=8 * MIB),
-    )(
-        at,
-        far(ocean_current.reshape(2, ROWS, LANES)),
-        far(wind_vector.reshape(2, ROWS * LANES)),
-        far(ice_cover.reshape(ROWS, LANES)),
-        far(flat),
-        far(speed),
-        far(route_slot),
     )
+    to_pair, to_next = edges(at, far(flat), far(speed), far(route_slot))
+    flat, speed = held(flat), held(speed)
     pairs = [(i, i + 1) for i in range(0, blocks, 2)]
     nexts = [(i, i + 1) for i in range(1, blocks - 1, 2)]
     got = held(lax.all_to_all(messages, BLK, 0, 0, tiled=True))
     from_next = held(lax.ppermute(to_next, BLK, nexts + [(j, i) for i, j in nexts]))
     from_pair = held(lax.ppermute(to_pair, BLK, pairs + [(j, i) for i, j in pairs]))
-    flat, speed = held(flat), held(speed)
-
-    moved, parts, cell = pl.pallas_call(
+    move = pl.pallas_call(
         lambda *refs: move_kernel(dirs, freqs, *refs),
-        out_shape=(pltpu.HBM((bins * ROWS, LANES), jnp.float32), near(bands, 48, LANES), near(48, LANES)),
-        in_specs=[smem, smem] + vmem_specs(6),
+        out_shape=(pltpu.HBM((bins * ROWS, LANES), jnp.float32), near(bands, 48, LANES), near(56, LANES)),
+        in_specs=[smem, smem] + vmem_specs(4),
         out_specs=(pl.BlockSpec(memory_space=pltpu.HBM), *vmem_specs(2)),
         scratch_shapes=[
             VMEM((LANES, LANES), jnp.float32),
             VMEM((freqs * ROWS, LANES), jnp.float32),
             VMEM((freqs * ROWS, LANES), jnp.float32),
             VMEM((freqs * ROWS, LANES), jnp.float32),
-            VMEM((freqs, LANES), jnp.float32),
-            VMEM((freqs, LANES), jnp.float32),
             VMEM((bins * ROWS, LANES), jnp.float32),
-            VMEM((bins + freqs + 8, LANES), jnp.float32),
-            VMEM((bins + freqs + 8, LANES), jnp.float32),
             pltpu.SemaphoreType.DMA((dirs,)),
         ],
         name="move",
         compiler_params=pltpu.CompilerParams(vmem_limit_bytes=8 * MIB),
-    )(at, trig, got, flat, speed, from_pair, from_next, route_slot)
+    )
+    moved, parts, cell = move(at, trig, got, flat, speed, route_slot)
+    parts, fixes = pl.pallas_call(
+        lambda *refs: fix_kernel(dirs, freqs, *refs),
+        out_shape=(near(bands, 48, LANES), near(2, bins, LANES)),
+        in_specs=[smem, smem] + vmem_specs(6),
+        out_specs=tuple(vmem_specs(2)),
+        scratch_shapes=[VMEM((bins + freqs + 8, LANES), jnp.float32), VMEM((bins + freqs + 8, LANES), jnp.float32)],
+        name="fix",
+        compiler_params=pltpu.CompilerParams(vmem_limit_bytes=4 * MIB),
+    )(at, trig, cell, from_pair, from_next, to_pair, to_next, parts)
 
     parts = held(lax.all_to_all(parts, DIR, 0, 0, tiled=True))
     damping, own = pl.pallas_call(
@@ -362,12 +415,12 @@
         lambda *refs: update_kernel(dirs, freqs, *refs),
         out_shape=f32(bins * ROWS, LANES),
         grid=(dirs,),
-        in_specs=[smem, smem, pl.BlockSpec((freqs * ROWS, LANES), lambda j: (j, 0))] + vmem_specs(2),
+        in_specs=[smem, smem, pl.BlockSpec((freqs * ROWS, LANES), lambda j: (j, 0))] + vmem_specs(3),
         out_specs=pl.BlockSpec((freqs * ROWS, LANES), lambda j: (j, 0)),
         name="update",
         compiler_params=pltpu.CompilerParams(vmem_limit_bytes=4 * MIB),
         cost_estimate=pl.CostEstimate(flops=3 * bins * ROWS * LANES, bytes_accessed=8 * bins * ROWS * LANES, transcendentals=0),
-    )(at, trig, pltpu.with_memory_space_constraint(moved, pltpu.HBM), cell, damping)
+    )(at, trig, pltpu.with_memory_space_constraint(moved, pltpu.HBM), cell, damping, fixes)
     ocean = pl.pallas_call(
         row_kernel,
         out_shape=f32(ROWS, LANES),

time: 72.2 us -> 73.2 us (1.014)
  Pallas kernels: 16.3 us -> 17.3 us
    pallas_call x2 -> x4, Pallas kernels: 8.37 us -> 9.32 us  [the longest x1 5.23 us: one_step(): moved, parts, cell = move(at, trig, got, flat, speed, route_slot)]
  transfers between devices with their start and end apart: 3 -> 3, of which waited for: 1 -> 1; matrix products, arithmetic and copies ran while one was open for 0% -> 0% of each run, Pallas kernels for 9% -> 18%
where the time goes in v1:
time: 73.2 us; the launch traced here: 72.8 us
  blocking collectives  32 us (44%)
  starting transfers between devices  17.7 us (24%)
  Pallas kernels  17.3 us (24%)
  waiting for transfers between devices  4.99 us (7%)
  between operations  0.75 us (1%)
    all_to_all x1, blocking collectives, one_step(): got = held(lax.all_to_all(messages, BLK, 0, 0, tiled=True))  23.5 us
    ppermute x1, starting transfers between devices, one_step(): lax.ppermute(to_pair, BLK, pairs + [(j, i) for i, j in pairs])  8.75 us
    all_to_all x1, blocking collectives, one_step(): parts = held(lax.all_to_all(parts, DIR, 0, 0, tiled=True))  8.47 us
    all_to_all x1, starting transfers between devices, one_step(): ocean = held(lax.all_to_all(own, BLK, 0, 0, tiled=True))  7.05 us
    pallas_call x1, Pallas kernels, one_step(): pl.pallas_call(lambda *refs: update_kernel(dirs, freqs, *refs), out_shape...  6.57 us
    pallas_call x1, Pallas kernels, one_step(): moved, parts, cell = move(at, trig, got, flat, speed, route_slot)  5.23 us
    all_to_all x1, waiting for transfers between devices, one_step(): ocean = held(lax.all_to_all(own, BLK, 0, 0, tiled=True))  4.98 us
    pallas_call x1, Pallas kernels, one_step(): to_pair, to_next = edges(at, far(flat), far(speed), far(route_slot))  2.14 us
  transfers between devices with their start and end apart: 3, of which 1 were waited for; matrix products, arithmetic and copies ran while one was open for 0% of the time, Pallas kernels for 18%

profile of v1, /device:TPU:1, one launch (start us, length us, event | category | flops | bytes accessed | tf_op | source)
XLA Modules:
  0.0 72.8 jit_solution(4724261612483343032)
XLA Ops:
  0.6 0.0 copy-start.3
  0.6 0.0 copy-start.2
  0.7 0.0 copy-start.1
  0.7 0.0 copy-start
  0.7 2.1 %edges.1 = (f32[368,128]{1,0:T(8,128)S(1)}, f32[368,128]{1,0:T(8,128)S(1)}) custom-call(s32[1]{0:T(128)} %bitcast.refs_0_.at_ref, f32[5184,128]{1,0:T(8,128)} %bitcast.16, f32[576,128]{1,0:T(8,128)} %bitcast.18, s32[16,128]{1,0:T(8,128)} %refs_3_.1), custom_call_target="tpu_custom_call" | custom-call | tf_op jit(solution)/shard_map/edges/pallas_call | solution.py:370
  2.8 8.7 %collective-permute-start = (f32[368,128]{1,0:T(8,128)S(1)}, f32[368,128]{1,0:T(8,128)S(1)}, u32[]{:S(2)}, u32[]{:S(2)}) collective-permute-start(f32[368,128]{1,0:T(8,128)S(1)} %get-tuple-element.13.refs_5_), channel_id=1, source_target_pairs={{0,4},{8,12},{16,20},{24,28},{32,36},{40,44},{48,52},{56,60},{64,6... | collective-permute-start | bytes 565256 | tf_op jit(solution)/shard_map/ppermute | solution.py:376
  11.6 1.9 %collective-permute-start.1 = (f32[368,128]{1,0:T(8,128)S(1)}, f32[368,128]{1,0:T(8,128)S(1)}, u32[]{:S(2)}, u32[]{:S(2)}) collective-permute-start(f32[368,128]{1,0:T(8,128)S(1)} %get-tuple-element.14.refs_6_), channel_id=1, source_target_pairs={{4,8},{12,16},{20,24},{28,32},{36,40},{44,48},{52,56},{60,64},{68,... | collective-permute-start | bytes 565256 | tf_op jit(solution)/shard_map/ppermute | solution.py:375
  13.5 1.0 %messages.1 = f32[128,128]{1,0:T(8,128)S(1)} custom-call(f32[2,16,128]{2,1,0:T(8,128)} %bitcast.24, f32[2,2048]{1,0:T(2,128)} %bitcast.25, f32[16,128]{1,0:T(8,128)} %bitcast.27), custom_call_target="tpu_custom_call" | custom-call | tf_op jit(solution)/shard_map/messages/pallas_call | solution.py:335
  14.5 23.5 %all_to_all.27 = f32[128,1,128]{2,1,0:T(1,128)S(1)} all-to-all(f32[128,1,128]{2,1,0:T(1,128)S(1)} %bitcast.22), channel_id=1, replica_groups=mesh['blk'=128,'dir'=4] {'blk'}, dimensions={0} | all-to-all | bytes 131072 | tf_op jit(solution)/shard_map/all_to_all | solution.py:374
  38.1 0.0 copy-done.3
  38.1 0.0 copy-done.2
  38.1 0.0 copy-done.1
  38.1 0.0 copy-done
  38.1 5.2 %move.1 = (f32[5184,128]{1,0:T(8,128)}, f32[4,48,128]{2,1,0:T(8,128)S(1)}, f32[56,128]{1,0:T(8,128)S(1)}) custom-call(s32[1]{0:T(128)} %bitcast.refs_0_.at_ref, f32[4,18]{1,0:T(4,128)S(1)} %copy-done.3, f32[128,128]{1,0:T(8,128)S(1)} %bitcast.20, f32[5184,128]{1,0:T(8,128)S(1)} %bitcast.17, f32[576,128]{1,0:T(8,128)S(1)} %bitcast.19, s32[16,128]{1,0:T(8,128)S(1)} %copy-done.2), custom_call_target="tpu_custom_call" | custom-call | tf_op jit(solution)/shard_map/move/pallas_call | solution.py:393
  43.3 0.0 collective-permute-done.refs_3_
  43.3 0.0 collective-permute-done.1.refs_4_
  43.4 0.9 %fix.1 = (f32[4,48,128]{2,1,0:T(8,128)S(1)}, f32[2,324,128]{2,1,0:T(8,128)S(1)}) custom-call(s32[1]{0:T(128)} %bitcast.refs_0_.at_ref, f32[4,18]{1,0:T(4,128)S(1)} %copy-done.3, f32[56,128]{1,0:T(8,128)S(1)} %get-tuple-element.12.refs_2_.refs_3_, f32[368,128]{1,0:T(8,128)S(1)} %collective-permute-done.refs_3_, ...), custom_call_target="tpu_custom_call" | custom-call | tf_op jit(solution)/shard_map/fix/pallas_call | solution.py:394
  44.3 8.5 %all_to_all.28.parts_ref = f32[4,48,128]{2,1,0:T(8,128)S(1)} all-to-all(f32[4,48,128]{2,1,0:T(8,128)S(1)} %get-tuple-element.16), channel_id=1, replica_groups=mesh['blk'=128,'dir'=4] {'dir'}, dimensions={0} | all-to-all | bytes 196608 | tf_op jit(solution)/shard_map/all_to_all | solution.py:404
  52.8 0.7 %forcing.1 = (f32[16,128]{1,0:T(8,128)S(1)}, f32[128,128]{1,0:T(8,128)}) custom-call(s32[1]{0:T(128)} %bitcast.refs_0_.at_ref, f32[4,48,128]{2,1,0:T(8,128)S(1)} %all_to_all.28.parts_ref), custom_call_target="tpu_custom_call" | custom-call | tf_op jit(solution)/shard_map/forcing/pallas_call | solution.py:405
  53.5 7.0 %all-to-all-start.2 = ((f32[128,1,128]{2,1,0:T(1,128)}), f32[128,1,128]{2,1,0:T(1,128)S(1)}, u32[]{:S(2)}, u32[]{:S(2)}) async-start(f32[128,1,128]{2,1,0:T(1,128)} %bitcast.11), calls=%async_computation.2 | async-start | bytes 131072 | tf_op jit(solution)/shard_map/all_to_all | solution.py:413
  60.5 6.6 %update.1 = f32[5184,128]{1,0:T(8,128)} custom-call(s32[1]{0:T(128)} %bitcast.refs_0_.at_ref, f32[4,18]{1,0:T(4,128)S(1)} %copy-done.3, f32[5184,128]{1,0:T(8,128)} %get-tuple-element.11.refs_2_, f32[56,128]{1,0:T(8,128)S(1)} %get-tuple-element.12.refs_2_.refs_3_, f32[16,128]{1,0:T(8,128)S(1)} %get-tuple-element.17.refs_4_, ...), custom_call_target="tpu_custom_call" | custom-call | flops 1990656 | bytes 5308416 | tf_op jit(solution)/shard_map/update/pallas_call | solution.py:414
  67.1 5.0 %all-to-all-done.2 = f32[128,1,128]{2,1,0:T(1,128)S(1)} async-done(((f32[128,1,128]{2,1,0:T(1,128)}), f32[128,1,128]{2,1,0:T(1,128)S(1)}, u32[]{:S(2)}, u32[]{:S(2)}) %all-to-all-start.2) | async-done | bytes 65568 | tf_op jit(solution)/shard_map/all_to_all | solution.py:413
  72.1 0.7 rows.1
Async XLA Ops:
  0.6 37.5 %copy-start.3 = (f32[4,18]{1,0:T(4,128)S(1)}, f32[4,18]{1,0:T(4,128)}, u32[]{:S(2)}) copy-start(f32[4,18]{1,0:T(4,128)} %constant.15.clone.refs_1_) | copy-start | bytes 868
  0.6 37.4 %copy-start.2 = (s32[16,128]{1,0:T(8,128)S(1)}, s32[16,128]{1,0:T(8,128)}, u32[]{:S(2)}) copy-start(s32[16,128]{1,0:T(8,128)} %refs_3_.1) | copy-start | bytes 24580
  0.7 37.4 %copy-start.1 = (f32[36,16,128]{2,1,0:T(8,128)S(1)}, f32[36,16,128]{2,1,0:T(8,128)}, u32[]{:S(2)}) copy-start(f32[36,16,128]{2,1,0:T(8,128)} %param.8) | copy-start | bytes 884740
  0.7 37.4 %copy-start = (f32[9,36,16,128]{3,2,1,0:T(8,128)S(1)}, f32[9,36,16,128]{3,2,1,0:T(8,128)}, u32[]{:S(2)}) copy-start(f32[9,36,16,128]{3,2,1,0:T(8,128)} %param.7) | copy-start | bytes 7962628
  2.8 40.5 %collective-permute-start = (f32[368,128]{1,0:T(8,128)S(1)}, f32[368,128]{1,0:T(8,128)S(1)}, u32[]{:S(2)}, u32[]{:S(2)}) collective-permute-start(f32[368,128]{1,0:T(8,128)S(1)} %get-tuple-element.13.refs_5_), channel_id=1, source_target_pairs={{0,4},{8,12},{16,20},{24,28},{32,36},{40,44},{48,52},{56,60},{64,6... | collective-permute-start | bytes 565256 | tf_op jit(solution)/shard_map/ppermute | solution.py:376
  11.6 31.8 %collective-permute-start.1 = (f32[368,128]{1,0:T(8,128)S(1)}, f32[368,128]{1,0:T(8,128)S(1)}, u32[]{:S(2)}, u32[]{:S(2)}) collective-permute-start(f32[368,128]{1,0:T(8,128)S(1)} %get-tuple-element.14.refs_6_), channel_id=1, source_target_pairs={{4,8},{12,16},{20,24},{28,32},{36,40},{44,48},{52,56},{60,64},{68,... | collective-permute-start | bytes 565256 | tf_op jit(solution)/shard_map/ppermute | solution.py:375
  53.5 18.6 %all-to-all-start.2 = ((f32[128,1,128]{2,1,0:T(1,128)}), f32[128,1,128]{2,1,0:T(1,128)S(1)}, u32[]{:S(2)}, u32[]{:S(2)}) async-start(f32[128,1,128]{2,1,0:T(1,128)} %bitcast.11), calls=%async_computation.2 | async-start | bytes 131072 | tf_op jit(solution)/shard_map/all_to_all | solution.py:413

commit v2 on v1

--- a/solution.py
+++ b/solution.py
@@ -37,22 +37,34 @@
     return lax.broadcasted_iota(jnp.int32, shape, len(shape) - 1)
 
 
-def message_kernel(
+def outgoing_kernel(
+    bins,
+    freqs,
+    at_ref,
     cur_hbm,
     wind_hbm,
     ice_hbm,
+    spec_hbm,
+    speed_hbm,
+    slot_hbm,
     out_ref,
+    pair_ref,
+    next_ref,
     cur_ref,
     wind_ref,
     ice_ref,
+    spec_ref,
+    speed_ref,
+    slot_ref,
     x_ref,
     sems,
 ):
-    sources, targets = (cur_hbm, wind_hbm, ice_hbm), (cur_ref, wind_ref, ice_ref)
+    sources = (cur_hbm, wind_hbm, ice_hbm, slot_hbm, speed_hbm, spec_hbm)
+    targets = (cur_ref, wind_ref, ice_ref, slot_ref, speed_ref, spec_ref)
     copies = [pltpu.make_async_copy(a, b, sems.at[i]) for i, (a, b) in enumerate(zip(sources, targets))]
     for copy in copies:
         copy.start()
-    for copy in copies:
+    for copy in copies[:3]:
         copy.wait()
     for c in range(2):
         for r in range(ROWS):
@@ -74,18 +86,9 @@
     after = pltpu.roll(pltpu.roll(whole, LANES - 1, 0), ROWS, 1)
     whole = jnp.where(wide == CUR_X, before, whole)
     out_ref[...] = jnp.where(wide == CUR_X + ROWS + 1, after, whole)
-
-
-def edge_kernel(
-    bins, freqs, at_ref, spec_hbm, speed_hbm, slot_hbm, pair_ref, next_ref, spec_ref, speed_ref, slot_ref, sems
-):
-    sources, targets = (slot_hbm, speed_hbm, spec_hbm), (slot_ref, speed_ref, spec_ref)
-    copies = [pltpu.make_async_copy(a, b, sems.at[i]) for i, (a, b) in enumerate(zip(sources, targets))]
-    for copy in copies:
-        copy.start()
-    for copy in copies:
+    odd = at_ref[0] >= BANDS
+    for copy in copies[3:]:
         copy.wait()
-    odd = at_ref[0] >= BANDS
 
     def trade(start, stop, first, last):
         pair_ref[start:stop, :] = jnp.where(odd, first, last)
@@ -332,42 +335,34 @@
     def far(value):
         return pltpu.with_memory_space_constraint(value, pltpu.HBM)
 
-    messages = pl.pallas_call(
-        message_kernel,
-        out_shape=near(LANES, LANES),
-        in_specs=[pl.BlockSpec(memory_space=pltpu.HBM)] * 3,
-        out_specs=vmem_specs(1)[0],
+    flat, speed = spectrum.reshape(bins * ROWS, LANES), group_speed.reshape(freqs * ROWS, LANES)
+    edge = near(bins + freqs + 8, LANES)
+    messages, to_pair, to_next = pl.pallas_call(
+        lambda *refs: outgoing_kernel(bins, freqs, *refs),
+        out_shape=(near(LANES, LANES), edge, edge),
+        in_specs=[smem] + [pl.BlockSpec(memory_space=pltpu.HBM)] * 6,
+        out_specs=tuple(vmem_specs(3)),
         scratch_shapes=[
             VMEM((2, ROWS, LANES), jnp.float32),
             VMEM((2, ROWS * LANES), jnp.float32),
             VMEM((ROWS, LANES), jnp.float32),
+            VMEM((bins * ROWS, LANES), jnp.float32),
+            VMEM((freqs * ROWS, LANES), jnp.float32),
+            VMEM((ROWS, LANES), jnp.int32),
             VMEM((2, ROWS, LANES), jnp.float32),
-            pltpu.SemaphoreType.DMA((3,)),
+            pltpu.SemaphoreType.DMA((6,)),
         ],
-        name="messages",
-        compiler_params=pltpu.CompilerParams(vmem_limit_bytes=4 * MIB),
+        name="outgoing",
+        compiler_params=pltpu.CompilerParams(vmem_limit_bytes=8 * MIB),
     )(
+        at,
         far(ocean_current.reshape(2, ROWS, LANES)),
         far(wind_vector.reshape(2, ROWS * LANES)),
         far(ice_cover.reshape(ROWS, LANES)),
+        far(flat),
+        far(speed),
+        far(route_slot),
     )
-    flat, speed = spectrum.reshape(bins * ROWS, LANES), group_speed.reshape(freqs * ROWS, LANES)
-    edge = near(bins + freqs + 8, LANES)
-    edges = pl.pallas_call(
-        lambda *refs: edge_kernel(bins, freqs, *refs),
-        out_shape=(edge, edge),
-        in_specs=[smem] + [pl.BlockSpec(memory_space=pltpu.HBM)] * 3,
-        out_specs=tuple(vmem_specs(2)),
-        scratch_shapes=[
-            VMEM((bins * ROWS, LANES), jnp.float32),
-            VMEM((freqs * ROWS, LANES), jnp.float32),
-            VMEM((ROWS, LANES), jnp.int32),
-            pltpu.SemaphoreType.DMA((3,)),
-        ],
-        name="edges",
-        compiler_params=pltpu.CompilerParams(vmem_limit_bytes=8 * MIB),
-    )
-    to_pair, to_next = edges(at, far(flat), far(speed), far(route_slot))
     flat, speed = held(flat), held(speed)
     pairs = [(i, i + 1) for i in range(0, blocks, 2)]
     nexts = [(i, i + 1) for i in range(1, blocks - 1, 2)]

time: 73.2 us -> 72.2 us (0.986)
  Pallas kernels: 17.3 us -> 16.4 us
    pallas_call x2 -> x1, Pallas kernels: 3.17 us -> 2.22 us  [one_step(): pl.pallas_call(lambda *refs: outgoing_kernel(bins, freqs, *refs), out_sha...]
  transfers between devices with their start and end apart: 3 -> 3, of which waited for: 1 -> 1; matrix products, arithmetic and copies ran while one was open for 0% -> 0% of each run, Pallas kernels for 18% -> 16%
where the time goes in v2:
time: 72.2 us; the launch traced here: 71.8 us
  blocking collectives  32 us (44%)
  starting transfers between devices  17.7 us (25%)
  Pallas kernels  16.4 us (23%)
  waiting for transfers between devices  4.99 us (7%)
  between operations  0.74 us (1%)
    all_to_all x1, blocking collectives, one_step(): got = held(lax.all_to_all(messages, BLK, 0, 0, tiled=True))  23.5 us
    ppermute x1, starting transfers between devices, one_step(): lax.ppermute(to_pair, BLK, pairs + [(j, i) for i, j in pairs])  8.75 us
    all_to_all x1, blocking collectives, one_step(): parts = held(lax.all_to_all(parts, DIR, 0, 0, tiled=True))  8.47 us
    all_to_all x1, starting transfers between devices, one_step(): ocean = held(lax.all_to_all(own, BLK, 0, 0, tiled=True))  7.05 us
    pallas_call x1, Pallas kernels, one_step(): pl.pallas_call(lambda *refs: update_kernel(dirs, freqs, *refs), out_shape...  6.57 us
    pallas_call x1, Pallas kernels, one_step(): moved, parts, cell = move(at, trig, got, flat, speed, route_slot)  5.23 us
    all_to_all x1, waiting for transfers between devices, one_step(): ocean = held(lax.all_to_all(own, BLK, 0, 0, tiled=True))  4.98 us
    pallas_call x1, Pallas kernels, one_step(): pl.pallas_call(lambda *refs: outgoing_kernel(bins, freqs, *refs), out_sha...  2.22 us
  transfers between devices with their start and end apart: 3, of which 1 were waited for; matrix products, arithmetic and copies ran while one was open for 0% of the time, Pallas kernels for 16%

profile of v2, /device:TPU:1, one launch (start us, length us, event | category | flops | bytes accessed | tf_op | source)
XLA Modules:
  0.0 71.8 jit_solution(5168802587644533520)
XLA Ops:
  0.6 0.0 copy-start.3
  0.6 0.0 copy-start.2
  0.7 0.0 copy-start.1
  0.7 0.0 copy-start
  0.7 2.2 %outgoing.1 = (f32[128,128]{1,0:T(8,128)S(1)}, f32[368,128]{1,0:T(8,128)S(1)}, f32[368,128]{1,0:T(8,128)S(1)}) custom-call(s32[1]{0:T(128)} %bitcast.refs_0_.at_ref, f32[2,16,128]{2,1,0:T(8,128)} %bitcast.24, f32[2,2048]{1,0:T(2,128)} %bitcast.25, f32[16,128]{1,0:T(8,128)} %bitcast.26, f32[5184,128]{1,0:T(8,128)} %bitcast.16, f32[576,128]{1,0:T(8,128)} %bitcast.18, ...), custom_call_target="tpu_custom_call" | custom-call | tf_op jit(solution)/shard_map/outgoing/pallas_call | solution.py:340
  2.9 8.7 %collective-permute-start = (f32[368,128]{1,0:T(8,128)S(1)}, f32[368,128]{1,0:T(8,128)S(1)}, u32[]{:S(2)}, u32[]{:S(2)}) collective-permute-start(f32[368,128]{1,0:T(8,128)S(1)} %get-tuple-element.15.refs_5_), channel_id=1, source_target_pairs={{0,4},{8,12},{16,20},{24,28},{32,36},{40,44},{48,52},{56,60},{64,6... | collective-permute-start | bytes 565256 | tf_op jit(solution)/shard_map/ppermute | solution.py:371
  11.7 1.9 %collective-permute-start.1 = (f32[368,128]{1,0:T(8,128)S(1)}, f32[368,128]{1,0:T(8,128)S(1)}, u32[]{:S(2)}, u32[]{:S(2)}) collective-permute-start(f32[368,128]{1,0:T(8,128)S(1)} %get-tuple-element.16.refs_6_), channel_id=1, source_target_pairs={{4,8},{12,16},{20,24},{28,32},{36,40},{44,48},{52,56},{60,64},{68,... | collective-permute-start | bytes 565256 | tf_op jit(solution)/shard_map/ppermute | solution.py:370
  13.6 23.5 %all_to_all.27 = f32[128,1,128]{2,1,0:T(1,128)S(1)} all-to-all(f32[128,1,128]{2,1,0:T(1,128)S(1)} %bitcast.22), channel_id=1, replica_groups=mesh['blk'=128,'dir'=4] {'blk'}, dimensions={0} | all-to-all | bytes 131072 | tf_op jit(solution)/shard_map/all_to_all | solution.py:369
  37.1 0.0 copy-done.3
  37.1 0.0 copy-done.2
  37.1 0.0 copy-done.1
  37.1 0.0 copy-done
  37.1 5.2 %move.1 = (f32[5184,128]{1,0:T(8,128)}, f32[4,48,128]{2,1,0:T(8,128)S(1)}, f32[56,128]{1,0:T(8,128)S(1)}) custom-call(s32[1]{0:T(128)} %bitcast.refs_0_.at_ref, f32[4,18]{1,0:T(4,128)S(1)} %copy-done.3, f32[128,128]{1,0:T(8,128)S(1)} %bitcast.20, f32[5184,128]{1,0:T(8,128)S(1)} %bitcast.17, f32[576,128]{1,0:T(8,128)S(1)} %bitcast.19, s32[16,128]{1,0:T(8,128)S(1)} %copy-done.2), custom_call_target="tpu_custom_call" | custom-call | tf_op jit(solution)/shard_map/move/pallas_call | solution.py:388
  42.4 0.0 collective-permute-done.refs_3_
  42.4 0.0 collective-permute-done.1.refs_4_
  42.4 0.9 %fix.1 = (f32[4,48,128]{2,1,0:T(8,128)S(1)}, f32[2,324,128]{2,1,0:T(8,128)S(1)}) custom-call(s32[1]{0:T(128)} %bitcast.refs_0_.at_ref, f32[4,18]{1,0:T(4,128)S(1)} %copy-done.3, f32[56,128]{1,0:T(8,128)S(1)} %get-tuple-element.14.refs_2_.refs_3_, f32[368,128]{1,0:T(8,128)S(1)} %collective-permute-done.refs_3_, ...), custom_call_target="tpu_custom_call" | custom-call | tf_op jit(solution)/shard_map/fix/pallas_call | solution.py:389
  43.3 8.5 %all_to_all.28.parts_ref = f32[4,48,128]{2,1,0:T(8,128)S(1)} all-to-all(f32[4,48,128]{2,1,0:T(8,128)S(1)} %get-tuple-element.18), channel_id=1, replica_groups=mesh['blk'=128,'dir'=4] {'dir'}, dimensions={0} | all-to-all | bytes 196608 | tf_op jit(solution)/shard_map/all_to_all | solution.py:399
  51.8 0.7 %forcing.1 = (f32[16,128]{1,0:T(8,128)S(1)}, f32[128,128]{1,0:T(8,128)}) custom-call(s32[1]{0:T(128)} %bitcast.refs_0_.at_ref, f32[4,48,128]{2,1,0:T(8,128)S(1)} %all_to_all.28.parts_ref), custom_call_target="tpu_custom_call" | custom-call | tf_op jit(solution)/shard_map/forcing/pallas_call | solution.py:400
  52.5 7.0 %all-to-all-start.2 = ((f32[128,1,128]{2,1,0:T(1,128)}), f32[128,1,128]{2,1,0:T(1,128)S(1)}, u32[]{:S(2)}, u32[]{:S(2)}) async-start(f32[128,1,128]{2,1,0:T(1,128)} %bitcast.11), calls=%async_computation.2 | async-start | bytes 131072 | tf_op jit(solution)/shard_map/all_to_all | solution.py:408
  59.6 6.6 %update.1 = f32[5184,128]{1,0:T(8,128)} custom-call(s32[1]{0:T(128)} %bitcast.refs_0_.at_ref, f32[4,18]{1,0:T(4,128)S(1)} %copy-done.3, f32[5184,128]{1,0:T(8,128)} %get-tuple-element.13.refs_2_, f32[56,128]{1,0:T(8,128)S(1)} %get-tuple-element.14.refs_2_.refs_3_, f32[16,128]{1,0:T(8,128)S(1)} %get-tuple-element.19.refs_4_, ...), custom_call_target="tpu_custom_call" | custom-call | flops 1990656 | bytes 5308416 | tf_op jit(solution)/shard_map/update/pallas_call | solution.py:409
  66.2 5.0 %all-to-all-done.2 = f32[128,1,128]{2,1,0:T(1,128)S(1)} async-done(((f32[128,1,128]{2,1,0:T(1,128)}), f32[128,1,128]{2,1,0:T(1,128)S(1)}, u32[]{:S(2)}, u32[]{:S(2)}) %all-to-all-start.2) | async-done | bytes 65568 | tf_op jit(solution)/shard_map/all_to_all | solution.py:408
  71.1 0.7 rows.1
Async XLA Ops:
  0.6 36.5 %copy-start.3 = (f32[4,18]{1,0:T(4,128)S(1)}, f32[4,18]{1,0:T(4,128)}, u32[]{:S(2)}) copy-start(f32[4,18]{1,0:T(4,128)} %constant.15.clone.refs_1_) | copy-start | bytes 868
  0.6 36.5 %copy-start.2 = (s32[16,128]{1,0:T(8,128)S(1)}, s32[16,128]{1,0:T(8,128)}, u32[]{:S(2)}) copy-start(s32[16,128]{1,0:T(8,128)} %refs_5_.1) | copy-start | bytes 24580
  0.7 36.5 %copy-start.1 = (f32[36,16,128]{2,1,0:T(8,128)S(1)}, f32[36,16,128]{2,1,0:T(8,128)}, u32[]{:S(2)}) copy-start(f32[36,16,128]{2,1,0:T(8,128)} %param.8) | copy-start | bytes 884740
  0.7 36.5 %copy-start = (f32[9,36,16,128]{3,2,1,0:T(8,128)S(1)}, f32[9,36,16,128]{3,2,1,0:T(8,128)}, u32[]{:S(2)}) copy-start(f32[9,36,16,128]{3,2,1,0:T(8,128)} %param.7) | copy-start | bytes 7962628
  2.9 39.5 %collective-permute-start = (f32[368,128]{1,0:T(8,128)S(1)}, f32[368,128]{1,0:T(8,128)S(1)}, u32[]{:S(2)}, u32[]{:S(2)}) collective-permute-start(f32[368,128]{1,0:T(8,128)S(1)} %get-tuple-element.15.refs_5_), channel_id=1, source_target_pairs={{0,4},{8,12},{16,20},{24,28},{32,36},{40,44},{48,52},{56,60},{64,6... | collective-permute-start | bytes 565256 | tf_op jit(solution)/shard_map/ppermute | solution.py:371
  11.7 30.7 %collective-permute-start.1 = (f32[368,128]{1,0:T(8,128)S(1)}, f32[368,128]{1,0:T(8,128)S(1)}, u32[]{:S(2)}, u32[]{:S(2)}) collective-permute-start(f32[368,128]{1,0:T(8,128)S(1)} %get-tuple-element.16.refs_6_), channel_id=1, source_target_pairs={{4,8},{12,16},{20,24},{28,32},{36,40},{44,48},{52,56},{60,64},{68,... | collective-permute-start | bytes 565256 | tf_op jit(solution)/shard_map/ppermute | solution.py:370
  52.5 18.6 %all-to-all-start.2 = ((f32[128,1,128]{2,1,0:T(1,128)}), f32[128,1,128]{2,1,0:T(1,128)S(1)}, u32[]{:S(2)}, u32[]{:S(2)}) async-start(f32[128,1,128]{2,1,0:T(1,128)} %bitcast.11), calls=%async_computation.2 | async-start | bytes 131072 | tf_op jit(solution)/shard_map/all_to_all | solution.py:408

commit v3 on v2

--- a/solution.py
+++ b/solution.py
@@ -24,7 +24,8 @@
 LANES = 128
 BANDS = 4
 MIB = 1 << 20
-UNROLL = 18
+FACES = 36
+PITCH = 24
 ROWS = 16
 CUR_X, CUR_Y, WIND_X, WIND_Y, ICE = 0, 24, 48, 64, 80
 
@@ -118,6 +119,7 @@
     sy_ref,
     sw_ref,
     moved_ref,
+    flux_ref,
     sems,
 ):
     shape = (ROWS, LANES)
@@ -139,6 +141,7 @@
     cur_y = turned_ref[CUR_Y : CUR_Y + ROWS, :]
     flow_y = open_y * (cur_y + next_y(cur_y))
     flow_w = pltpu.roll(flow_y, 1, 1)
+    open_w = pltpu.roll(open_y, 1, 1)
 
     owner, place = jnp.maximum(slots, 0) // 16, jnp.where(slots >= 0, slots % 16, -1)
     wind_x, wind_y, ice = (jnp.zeros(shape, jnp.float32) for _ in range(3))
@@ -154,6 +157,7 @@
     cell_ref[0:16, :] = wind_x
     cell_ref[16:32, :] = wind_y
     cell_ref[32:48, :] = gain
+    cell_ref[56:72, :] = sea
     for side, x in enumerate((CUR_X, CUR_X + ROWS)):
         cell_ref[48 + side : 49 + side, :] = turned_ref[x : x + 1, :] + turned_ref[x + 1 : x + 2, :]
 
@@ -161,63 +165,65 @@
         base = pl.multiple_of(k * ROWS, ROWS)
         speed = speed_ref[pl.ds(base, ROWS), :]
         sx_ref[pl.ds(base, ROWS), :] = open_x * (speed + shifted_down(speed))
-        side = open_y * (speed + next_y(speed))
-        sy_ref[pl.ds(base, ROWS), :] = side
-        sw_ref[pl.ds(base, ROWS), :] = pltpu.roll(side, 1, 1)
+        sy_ref[pl.ds(base, ROWS), :] = open_y * (speed + next_y(speed))
+        sw_ref[pl.ds(base, ROWS), :] = open_w * (speed + pltpu.roll(speed, 1, 1))
         return 0
 
-    lax.fori_loop(0, freqs, faces, 0, unroll=12)
+    lax.fori_loop(0, freqs, faces, 0, unroll=FACES)
 
     zero = jnp.zeros(shape, jnp.float32)
-    moment, stress_x, stress_y, drift_x, drift_y, damp_x, damp_y = (zero,) * 7
+    for k in range(freqs):
+        flux_ref[k * PITCH + ROWS : (k + 1) * PITCH, :] = jnp.zeros((PITCH - ROWS, LANES), jnp.float32)
     at = at_ref[0] % BANDS
-    copies = []
-    for j in range(dirs):
+
+    def out_copy(j):
+        part = pl.ds(pl.multiple_of(j * (freqs * ROWS), ROWS), freqs * ROWS)
+        return pltpu.make_async_copy(moved_ref.at[part, :], stored_ref.at[part, :], sems.at[j])
+
+    def direction(j, sums):
+        moment, stress_x, stress_y, drift_x, drift_y, damp_x, damp_y = sums
         cosine, sine = trig_ref[at, j], trig_ref[at, dirs + j]
-
-        def step(k, sums):
-            second, third, fourth = sums
-            base = pl.multiple_of(k * ROWS, ROWS)
-            here = pl.multiple_of(j * freqs * ROWS + k * ROWS, ROWS)
-            energy = spec_ref[pl.ds(here, ROWS), :]
-            u = sx_ref[pl.ds(base, ROWS), :] * cosine + flow_x
-            below = u * jnp.where(u > 0.0, shifted_down(energy), energy)
-            above = pltpu.roll(below, ROWS - 1, 0)
-            v = sy_ref[pl.ds(base, ROWS), :] * sine + flow_y
+        start = pl.multiple_of(j * (freqs * ROWS), ROWS)
+        second, third, fourth = zero, zero, zero
+        for k in range(freqs):
+            face = slice(k * ROWS, (k + 1) * ROWS)
+            energy = spec_ref[pl.ds(start + k * ROWS, ROWS), :]
+            lower = shifted_down(energy) if k == 0 else spec_ref[pl.ds(start + (k * ROWS - 1), ROWS), :]
+            u = sx_ref[face, :] * cosine + flow_x
+            below = u * jnp.where(u > 0.0, lower, energy)
+            flux_ref[k * PITCH : k * PITCH + ROWS, :] = below
+            above = flux_ref[k * PITCH + 1 : k * PITCH + ROWS + 1, :]
+            v = sy_ref[face, :] * sine + flow_y
             right = v * jnp.where(v > 0.0, energy, next_y(energy))
-            w = sw_ref[pl.ds(base, ROWS), :] * sine + flow_w
+            w = sw_ref[face, :] * sine + flow_w
             left = w * jnp.where(w > 0.0, pltpu.roll(energy, 1, 1), energy)
-            moved = sea * (energy - ((above - below) + (right - left)))
-            moved_ref[pl.ds(here, ROWS), :] = moved
-            return (
-                second * (RATIO_STEP**-2) + moved,
-                third * (RATIO_STEP**-3) + moved,
-                fourth * (RATIO_STEP**-4) + moved,
-            )
-
-        def out_copy():
-            part = pl.ds(j * freqs * ROWS, freqs * ROWS)
-            return pltpu.make_async_copy(moved_ref.at[part, :], stored_ref.at[part, :], sems.at[j])
-
-        second, third, fourth = lax.fori_loop(0, freqs, step, (zero, zero, zero), unroll=UNROLL)
-        copies.append(out_copy())
-        copies[-1].start()
+            moved = energy - ((above - below) + (right - left))
+            moved_ref[pl.ds(start + k * ROWS, ROWS), :] = moved
+            second = second * (RATIO_STEP**-2) + moved
+            third = third * (RATIO_STEP**-3) + moved
+            fourth = fourth * (RATIO_STEP**-4) + moved
+        out_copy(j).start()
+        second, third, fourth = sea * second, sea * third, sea * fourth
         wind_gain = gain * jnp.maximum(wind_x * cosine + wind_y * sine, 0.0)
         push = wind_gain * second
         drift = third + wind_gain * fourth
-        moment += second
-        stress_x += cosine * push
-        stress_y += sine * push
-        drift_x += cosine * drift
-        drift_y += sine * drift
-        damp_x += cosine * fourth
-        damp_y += sine * fourth
+        return (
+            moment + second,
+            stress_x + cosine * push,
+            stress_y + sine * push,
+            drift_x + cosine * drift,
+            drift_y + sine * drift,
+            damp_x + cosine * fourth,
+            damp_y + sine * fourth,
+        )
+
+    moment, stress_x, stress_y, drift_x, drift_y, damp_x, damp_y = lax.fori_loop(0, dirs, direction, (zero,) * 7)
     for c, (main, damped) in enumerate(((stress_x, zero), (stress_y, zero), (drift_x, damp_x), (drift_y, damp_y))):
         parts_ref[c, 0:16, :] = moment
         parts_ref[c, 16:32, :] = main
         parts_ref[c, 32:48, :] = damped
-    for copy in copies:
-        copy.wait()
+    for j in range(dirs):
+        out_copy(j).wait()
 
 
 def fix_kernel(
@@ -292,14 +298,15 @@
     j, at = pl.program_id(0), at_ref[0] % BANDS
     cosine, sine = trig_ref[at, j], trig_ref[at, dirs + j]
     wind = jnp.maximum(cell_ref[0:16, :] * cosine + cell_ref[16:32, :] * sine, 0.0)
-    growth = cell_ref[32:48, :] * wind - damping_ref[...]
+    sea = cell_ref[56:72, :]
+    growth = sea * (cell_ref[32:48, :] * wind - damping_ref[...])
     row = lax.broadcasted_iota(jnp.int32, (ROWS, LANES), 0)
     for k in range(freqs):
         ratio = RATIO_STEP ** (k - freqs + 1)
         first, last = (jnp.broadcast_to(fix_ref[side, pl.ds(j * freqs + k, 1), :], (ROWS, LANES)) for side in (0, 1))
         edge = jnp.where(row == 0, first, jnp.where(row == ROWS - 1, last, 0.0))
         moved = moved_ref[k * ROWS : (k + 1) * ROWS, :] + edge
-        out_ref[k * ROWS : (k + 1) * ROWS, :] = moved * (1.0 + ratio * growth)
+        out_ref[k * ROWS : (k + 1) * ROWS, :] = moved * (sea + ratio * growth)
 
 
 def row_kernel(got_ref, out_ref):
@@ -371,7 +378,7 @@
     from_pair = held(lax.ppermute(to_pair, BLK, pairs + [(j, i) for i, j in pairs]))
     move = pl.pallas_call(
         lambda *refs: move_kernel(dirs, freqs, *refs),
-        out_shape=(pltpu.HBM((bins * ROWS, LANES), jnp.float32), near(bands, 48, LANES), near(56, LANES)),
+        out_shape=(pltpu.HBM((bins * ROWS, LANES), jnp.float32), near(bands, 48, LANES), near(72, LANES)),
         in_specs=[smem, smem] + vmem_specs(4),
         out_specs=(pl.BlockSpec(memory_space=pltpu.HBM), *vmem_specs(2)),
         scratch_shapes=[
@@ -380,6 +387,7 @@
             VMEM((freqs * ROWS, LANES), jnp.float32),
             VMEM((freqs * ROWS, LANES), jnp.float32),
             VMEM((bins * ROWS, LANES), jnp.float32),
+            VMEM((freqs * PITCH, LANES), jnp.float32),
             pltpu.SemaphoreType.DMA((dirs,)),
         ],
         name="move",

time: 72.2 us -> 71.6 us (level)
  no operation moved by 1% of the time
where the time goes in v3:
time: 71.6 us; the launch traced here: 71.2 us
  blocking collectives  32 us (45%)
  starting transfers between devices  17.7 us (25%)
  Pallas kernels  15.8 us (22%)
  waiting for transfers between devices  4.99 us (7%)
  between operations  0.74 us (1%)
    all_to_all x1, blocking collectives, one_step(): got = held(lax.all_to_all(messages, BLK, 0, 0, tiled=True))  23.5 us
    ppermute x1, starting transfers between devices, one_step(): lax.ppermute(to_pair, BLK, pairs + [(j, i) for i, j in pairs])  8.75 us
    all_to_all x1, blocking collectives, one_step(): parts = held(lax.all_to_all(parts, DIR, 0, 0, tiled=True))  8.47 us
    all_to_all x1, starting transfers between devices, one_step(): ocean = held(lax.all_to_all(own, BLK, 0, 0, tiled=True))  7.05 us
    pallas_call x1, Pallas kernels, one_step(): pl.pallas_call(lambda *refs: update_kernel(dirs, freqs, *refs), out_shape...  6.57 us
    all_to_all x1, waiting for transfers between devices, one_step(): ocean = held(lax.all_to_all(own, BLK, 0, 0, tiled=True))  4.99 us
    pallas_call x1, Pallas kernels, one_step(): moved, parts, cell = move(at, trig, got, flat, speed, route_slot)  4.63 us
    pallas_call x1, Pallas kernels, one_step(): pl.pallas_call(lambda *refs: outgoing_kernel(bins, freqs, *refs), out_sha...  2.22 us
  transfers between devices with their start and end apart: 3, of which 1 were waited for; matrix products, arithmetic and copies ran while one was open for 0% of the time, Pallas kernels for 16%

profile of v3, /device:TPU:1, one launch (start us, length us, event | category | flops | bytes accessed | tf_op | source)
XLA Modules:
  0.0 71.2 jit_solution(12773704213094504474)
XLA Ops:
  0.6 0.0 copy-start.3
  0.6 0.0 copy-start.2
  0.7 0.0 copy-start.1
  0.7 0.0 copy-start
  0.7 2.2 %outgoing.1 = (f32[128,128]{1,0:T(8,128)S(1)}, f32[368,128]{1,0:T(8,128)S(1)}, f32[368,128]{1,0:T(8,128)S(1)}) custom-call(s32[1]{0:T(128)} %bitcast.refs_0_.at_ref, f32[2,16,128]{2,1,0:T(8,128)} %bitcast.24, f32[2,2048]{1,0:T(2,128)} %bitcast.25, f32[16,128]{1,0:T(8,128)} %bitcast.26, f32[5184,128]{1,0:T(8,128)} %bitcast.16, f32[576,128]{1,0:T(8,128)} %bitcast.18, ...), custom_call_target="tpu_custom_call" | custom-call | tf_op jit(solution)/shard_map/outgoing/pallas_call | solution.py:347
  2.9 8.7 %collective-permute-start = (f32[368,128]{1,0:T(8,128)S(1)}, f32[368,128]{1,0:T(8,128)S(1)}, u32[]{:S(2)}, u32[]{:S(2)}) collective-permute-start(f32[368,128]{1,0:T(8,128)S(1)} %get-tuple-element.15.refs_5_), channel_id=1, source_target_pairs={{0,4},{8,12},{16,20},{24,28},{32,36},{40,44},{48,52},{56,60},{64,6... | collective-permute-start | bytes 565256 | tf_op jit(solution)/shard_map/ppermute | solution.py:378
  11.7 1.9 %collective-permute-start.1 = (f32[368,128]{1,0:T(8,128)S(1)}, f32[368,128]{1,0:T(8,128)S(1)}, u32[]{:S(2)}, u32[]{:S(2)}) collective-permute-start(f32[368,128]{1,0:T(8,128)S(1)} %get-tuple-element.16.refs_6_), channel_id=1, source_target_pairs={{4,8},{12,16},{20,24},{28,32},{36,40},{44,48},{52,56},{60,64},{68,... | collective-permute-start | bytes 565256 | tf_op jit(solution)/shard_map/ppermute | solution.py:377
  13.6 23.5 %all_to_all.27 = f32[128,1,128]{2,1,0:T(1,128)S(1)} all-to-all(f32[128,1,128]{2,1,0:T(1,128)S(1)} %bitcast.22), channel_id=1, replica_groups=mesh['blk'=128,'dir'=4] {'blk'}, dimensions={0} | all-to-all | bytes 131072 | tf_op jit(solution)/shard_map/all_to_all | solution.py:376
  37.1 0.0 copy-done.3
  37.1 0.0 copy-done.2
  37.1 0.0 copy-done.1
  37.1 0.0 copy-done
  37.1 4.6 %move.1 = (f32[5184,128]{1,0:T(8,128)}, f32[4,48,128]{2,1,0:T(8,128)S(1)}, f32[72,128]{1,0:T(8,128)S(1)}) custom-call(s32[1]{0:T(128)} %bitcast.refs_0_.at_ref, f32[4,18]{1,0:T(4,128)S(1)} %copy-done.3, f32[128,128]{1,0:T(8,128)S(1)} %bitcast.20, f32[5184,128]{1,0:T(8,128)S(1)} %bitcast.17, f32[576,128]{1,0:T(8,128)S(1)} %bitcast.19, s32[16,128]{1,0:T(8,128)S(1)} %copy-done.2), custom_call_target="tpu_custom_call" | custom-call | tf_op jit(solution)/shard_map/move/pallas_call | solution.py:396
  41.8 0.0 collective-permute-done.refs_3_
  41.8 0.0 collective-permute-done.1.refs_4_
  41.8 0.9 %fix.1 = (f32[4,48,128]{2,1,0:T(8,128)S(1)}, f32[2,324,128]{2,1,0:T(8,128)S(1)}) custom-call(s32[1]{0:T(128)} %bitcast.refs_0_.at_ref, f32[4,18]{1,0:T(4,128)S(1)} %copy-done.3, f32[72,128]{1,0:T(8,128)S(1)} %get-tuple-element.14.refs_2_.refs_3_, f32[368,128]{1,0:T(8,128)S(1)} %collective-permute-done.refs_3_, ...), custom_call_target="tpu_custom_call" | custom-call | tf_op jit(solution)/shard_map/fix/pallas_call | solution.py:397
  42.7 8.5 %all_to_all.28.parts_ref = f32[4,48,128]{2,1,0:T(8,128)S(1)} all-to-all(f32[4,48,128]{2,1,0:T(8,128)S(1)} %get-tuple-element.18), channel_id=1, replica_groups=mesh['blk'=128,'dir'=4] {'dir'}, dimensions={0} | all-to-all | bytes 196608 | tf_op jit(solution)/shard_map/all_to_all | solution.py:407
  51.2 0.7 %forcing.1 = (f32[16,128]{1,0:T(8,128)S(1)}, f32[128,128]{1,0:T(8,128)}) custom-call(s32[1]{0:T(128)} %bitcast.refs_0_.at_ref, f32[4,48,128]{2,1,0:T(8,128)S(1)} %all_to_all.28.parts_ref), custom_call_target="tpu_custom_call" | custom-call | tf_op jit(solution)/shard_map/forcing/pallas_call | solution.py:408
  51.9 7.0 %all-to-all-start.2 = ((f32[128,1,128]{2,1,0:T(1,128)}), f32[128,1,128]{2,1,0:T(1,128)S(1)}, u32[]{:S(2)}, u32[]{:S(2)}) async-start(f32[128,1,128]{2,1,0:T(1,128)} %bitcast.11), calls=%async_computation.2 | async-start | bytes 131072 | tf_op jit(solution)/shard_map/all_to_all | solution.py:416
  59.0 6.6 %update.1 = f32[5184,128]{1,0:T(8,128)} custom-call(s32[1]{0:T(128)} %bitcast.refs_0_.at_ref, f32[4,18]{1,0:T(4,128)S(1)} %copy-done.3, f32[5184,128]{1,0:T(8,128)} %get-tuple-element.13.refs_2_, f32[72,128]{1,0:T(8,128)S(1)} %get-tuple-element.14.refs_2_.refs_3_, f32[16,128]{1,0:T(8,128)S(1)} %get-tuple-element.19.refs_4_, ...), custom_call_target="tpu_custom_call" | custom-call | flops 1990656 | bytes 5308416 | tf_op jit(solution)/shard_map/update/pallas_call | solution.py:417
  65.6 5.0 %all-to-all-done.2 = f32[128,1,128]{2,1,0:T(1,128)S(1)} async-done(((f32[128,1,128]{2,1,0:T(1,128)}), f32[128,1,128]{2,1,0:T(1,128)S(1)}, u32[]{:S(2)}, u32[]{:S(2)}) %all-to-all-start.2) | async-done | bytes 65568 | tf_op jit(solution)/shard_map/all_to_all | solution.py:416
  70.5 0.7 rows.1
Async XLA Ops:
  0.6 36.5 %copy-start.3 = (f32[4,18]{1,0:T(4,128)S(1)}, f32[4,18]{1,0:T(4,128)}, u32[]{:S(2)}) copy-start(f32[4,18]{1,0:T(4,128)} %constant.15.clone.refs_1_) | copy-start | bytes 868
  0.6 36.5 %copy-start.2 = (s32[16,128]{1,0:T(8,128)S(1)}, s32[16,128]{1,0:T(8,128)}, u32[]{:S(2)}) copy-start(s32[16,128]{1,0:T(8,128)} %refs_5_.1) | copy-start | bytes 24580
  0.7 36.5 %copy-start.1 = (f32[36,16,128]{2,1,0:T(8,128)S(1)}, f32[36,16,128]{2,1,0:T(8,128)}, u32[]{:S(2)}) copy-start(f32[36,16,128]{2,1,0:T(8,128)} %param.8) | copy-start | bytes 884740
  0.7 36.5 %copy-start = (f32[9,36,16,128]{3,2,1,0:T(8,128)S(1)}, f32[9,36,16,128]{3,2,1,0:T(8,128)}, u32[]{:S(2)}) copy-start(f32[9,36,16,128]{3,2,1,0:T(8,128)} %param.7) | copy-start | bytes 7962628
  2.9 38.9 %collective-permute-start = (f32[368,128]{1,0:T(8,128)S(1)}, f32[368,128]{1,0:T(8,128)S(1)}, u32[]{:S(2)}, u32[]{:S(2)}) collective-permute-start(f32[368,128]{1,0:T(8,128)S(1)} %get-tuple-element.15.refs_5_), channel_id=1, source_target_pairs={{0,4},{8,12},{16,20},{24,28},{32,36},{40,44},{48,52},{56,60},{64,6... | collective-permute-start | bytes 565256 | tf_op jit(solution)/shard_map/ppermute | solution.py:378
  11.7 30.1 %collective-permute-start.1 = (f32[368,128]{1,0:T(8,128)S(1)}, f32[368,128]{1,0:T(8,128)S(1)}, u32[]{:S(2)}, u32[]{:S(2)}) collective-permute-start(f32[368,128]{1,0:T(8,128)S(1)} %get-tuple-element.16.refs_6_), channel_id=1, source_target_pairs={{4,8},{12,16},{20,24},{28,32},{36,40},{44,48},{52,56},{60,64},{68,... | collective-permute-start | bytes 565256 | tf_op jit(solution)/shard_map/ppermute | solution.py:377
  51.9 18.6 %all-to-all-start.2 = ((f32[128,1,128]{2,1,0:T(1,128)}), f32[128,1,128]{2,1,0:T(1,128)S(1)}, u32[]{:S(2)}, u32[]{:S(2)}) async-start(f32[128,1,128]{2,1,0:T(1,128)} %bitcast.11), calls=%async_computation.2 | async-start | bytes 131072 | tf_op jit(solution)/shard_map/all_to_all | solution.py:416

commit v4 on v3

--- a/solution.py
+++ b/solution.py
@@ -48,16 +48,17 @@
     spec_hbm,
     speed_hbm,
     slot_hbm,
-    out_ref,
+    sent_hbm,
     pair_ref,
     next_ref,
+    spec_ref,
+    speed_ref,
     cur_ref,
     wind_ref,
     ice_ref,
-    spec_ref,
-    speed_ref,
     slot_ref,
     x_ref,
+    out_ref,
     sems,
 ):
     sources = (cur_hbm, wind_hbm, ice_hbm, slot_hbm, speed_hbm, spec_hbm)
@@ -87,6 +88,8 @@
     after = pltpu.roll(pltpu.roll(whole, LANES - 1, 0), ROWS, 1)
     whole = jnp.where(wide == CUR_X, before, whole)
     out_ref[...] = jnp.where(wide == CUR_X + ROWS + 1, after, whole)
+    sending = pltpu.make_async_copy(out_ref, sent_hbm, sems.at[len(sources)])
+    sending.start()
     odd = at_ref[0] >= BANDS
     for copy in copies[3:]:
         copy.wait()
@@ -100,6 +103,7 @@
     sea = jnp.where(slot_ref[...] >= 0, 1.0, 0.0)
     sea = [jnp.broadcast_to(sea[r : r + 1, :], (8, LANES)) for r in (0, ROWS - 1)]
     trade(bins + freqs, bins + freqs + 8, *sea)
+    sending.wait()
 
 
 def move_kernel(
@@ -344,20 +348,25 @@
 
     flat, speed = spectrum.reshape(bins * ROWS, LANES), group_speed.reshape(freqs * ROWS, LANES)
     edge = near(bins + freqs + 8, LANES)
-    messages, to_pair, to_next = pl.pallas_call(
+    messages, to_pair, to_next, flat, speed = pl.pallas_call(
         lambda *refs: outgoing_kernel(bins, freqs, *refs),
-        out_shape=(near(LANES, LANES), edge, edge),
+        out_shape=(
+            pltpu.HBM((LANES, LANES), jnp.float32),
+            edge,
+            edge,
+            near(bins * ROWS, LANES),
+            near(freqs * ROWS, LANES),
+        ),
         in_specs=[smem] + [pl.BlockSpec(memory_space=pltpu.HBM)] * 6,
-        out_specs=tuple(vmem_specs(3)),
+        out_specs=(pl.BlockSpec(memory_space=pltpu.HBM), *vmem_specs(4)),
         scratch_shapes=[
             VMEM((2, ROWS, LANES), jnp.float32),
             VMEM((2, ROWS * LANES), jnp.float32),
             VMEM((ROWS, LANES), jnp.float32),
-            VMEM((bins * ROWS, LANES), jnp.float32),
-            VMEM((freqs * ROWS, LANES), jnp.float32),
             VMEM((ROWS, LANES), jnp.int32),
             VMEM((2, ROWS, LANES), jnp.float32),
-            pltpu.SemaphoreType.DMA((6,)),
+            VMEM((LANES, LANES), jnp.float32),
+            pltpu.SemaphoreType.DMA((7,)),
         ],
         name="outgoing",
         compiler_params=pltpu.CompilerParams(vmem_limit_bytes=8 * MIB),
@@ -370,7 +379,6 @@
         far(speed),
         far(route_slot),
     )
-    flat, speed = held(flat), held(speed)
     pairs = [(i, i + 1) for i in range(0, blocks, 2)]
     nexts = [(i, i + 1) for i in range(1, blocks - 1, 2)]
     got = held(lax.all_to_all(messages, BLK, 0, 0, tiled=True))

time: 71.6 us -> 72 us (level)
  no operation moved by 1% of the time
where the time goes in v4:
time: 72 us; the launch traced here: 71.5 us
  blocking collectives  32.1 us (45%)
  starting transfers between devices  17.8 us (25%)
  Pallas kernels  15.8 us (22%)
  waiting for transfers between devices  5.04 us (7%)
  between operations  0.72 us (1%)
    all_to_all x1, blocking collectives, one_step(): got = held(lax.all_to_all(messages, BLK, 0, 0, tiled=True))  23.7 us
    ppermute x1, starting transfers between devices, one_step(): lax.ppermute(to_pair, BLK, pairs + [(j, i) for i, j in pairs])  8.75 us
    all_to_all x1, blocking collectives, one_step(): parts = held(lax.all_to_all(parts, DIR, 0, 0, tiled=True))  8.47 us
    all_to_all x1, starting transfers between devices, one_step(): ocean = held(lax.all_to_all(own, BLK, 0, 0, tiled=True))  7.12 us
    pallas_call x1, Pallas kernels, one_step(): pl.pallas_call(lambda *refs: update_kernel(dirs, freqs, *refs), out_shape...  6.57 us
    all_to_all x1, waiting for transfers between devices, one_step(): ocean = held(lax.all_to_all(own, BLK, 0, 0, tiled=True))  5.04 us
    pallas_call x1, Pallas kernels, one_step(): moved, parts, cell = move(at, trig, got, flat, speed, route_slot)  4.81 us
    pallas_call x1, Pallas kernels, one_step(): pl.pallas_call(lambda *refs: outgoing_kernel(bins, freqs, *refs), out_sha...  2.09 us
  transfers between devices with their start and end apart: 3, of which 1 were waited for; matrix products, arithmetic and copies ran while one was open for 0% of the time, Pallas kernels for 16%

profile of v4, /device:TPU:1, one launch (start us, length us, event | category | flops | bytes accessed | tf_op | source)
XLA Modules:
  0.0 71.5 jit_solution(15870451296259228154)
XLA Ops:
  0.6 0.0 copy-start.1
  0.6 0.0 copy-start
  0.7 2.1 %outgoing.1 = (f32[128,128]{1,0:T(8,128)}, f32[368,128]{1,0:T(8,128)S(1)}, f32[368,128]{1,0:T(8,128)S(1)}, f32[5184,128]{1,0:T(8,128)S(1)}, f32[576,128]{1,0:T(8,128)S(1)}) custom-call(s32[1]{0:T(128)} %bitcast.refs_0_.at_ref, f32[2,16,128]{2,1,0:T(8,128)} %bitcast.22, f32[2,2048]{1,0:T(2,128)} %bitcast.23, f32[16,128]{1,0:T(8,128)} %bitcast.24, ...), custom_call_target="tpu_custom_call" | custom-call | tf_op jit(solution)/shard_map/outgoing/pallas_call | solution.py:351
  2.8 8.7 %collective-permute-start = (f32[368,128]{1,0:T(8,128)S(1)}, f32[368,128]{1,0:T(8,128)S(1)}, u32[]{:S(2)}, u32[]{:S(2)}) collective-permute-start(f32[368,128]{1,0:T(8,128)S(1)} %get-tuple-element.19.refs_5_), channel_id=1, source_target_pairs={{0,4},{8,12},{16,20},{24,28},{32,36},{40,44},{48,52},{56,60},{64,6... | collective-permute-start | bytes 565256 | tf_op jit(solution)/shard_map/ppermute | solution.py:386
  11.5 1.9 %collective-permute-start.1 = (f32[368,128]{1,0:T(8,128)S(1)}, f32[368,128]{1,0:T(8,128)S(1)}, u32[]{:S(2)}, u32[]{:S(2)}) collective-permute-start(f32[368,128]{1,0:T(8,128)S(1)} %get-tuple-element.20.refs_6_), channel_id=1, source_target_pairs={{4,8},{12,16},{20,24},{28,32},{36,40},{44,48},{52,56},{60,64},{68,... | collective-permute-start | bytes 565256 | tf_op jit(solution)/shard_map/ppermute | solution.py:385
  13.4 23.7 %all_to_all.27 = f32[128,1,128]{2,1,0:T(1,128)S(1)} all-to-all(f32[128,1,128]{2,1,0:T(1,128)} %bitcast.21), channel_id=1, replica_groups=mesh['blk'=128,'dir'=4] {'blk'}, dimensions={0} | all-to-all | bytes 131072 | tf_op jit(solution)/shard_map/all_to_all | solution.py:384
  37.1 0.0 copy-done.1
  37.1 0.0 copy-done
  37.1 4.8 %move.1 = (f32[5184,128]{1,0:T(8,128)}, f32[4,48,128]{2,1,0:T(8,128)S(1)}, f32[72,128]{1,0:T(8,128)S(1)}) custom-call(s32[1]{0:T(128)} %bitcast.refs_0_.at_ref, f32[4,18]{1,0:T(4,128)S(1)} %copy-done.1, f32[128,128]{1,0:T(8,128)S(1)} %bitcast.16, f32[5184,128]{1,0:T(8,128)S(1)} %get-tuple-element.15.refs_3_, f32[576,128]{1,0:T(8,128)S(1)} %get-tuple-element.16.refs_4_, ...), custom_call_target="tpu_custom_call" | custom-call | tf_op jit(solution)/shard_map/move/pallas_call | solution.py:404
  41.9 0.0 collective-permute-done.refs_3_
  41.9 0.0 collective-permute-done.1.refs_4_
  41.9 0.9 %fix.1 = (f32[4,48,128]{2,1,0:T(8,128)S(1)}, f32[2,324,128]{2,1,0:T(8,128)S(1)}) custom-call(s32[1]{0:T(128)} %bitcast.refs_0_.at_ref, f32[4,18]{1,0:T(4,128)S(1)} %copy-done.1, f32[72,128]{1,0:T(8,128)S(1)} %get-tuple-element.18.refs_2_.refs_3_, f32[368,128]{1,0:T(8,128)S(1)} %collective-permute-done.refs_3_, ...), custom_call_target="tpu_custom_call" | custom-call | tf_op jit(solution)/shard_map/fix/pallas_call | solution.py:405
  42.9 8.5 %all_to_all.28.parts_ref = f32[4,48,128]{2,1,0:T(8,128)S(1)} all-to-all(f32[4,48,128]{2,1,0:T(8,128)S(1)} %get-tuple-element.22), channel_id=1, replica_groups=mesh['blk'=128,'dir'=4] {'dir'}, dimensions={0} | all-to-all | bytes 196608 | tf_op jit(solution)/shard_map/all_to_all | solution.py:415
  51.3 0.7 %forcing.1 = (f32[16,128]{1,0:T(8,128)S(1)}, f32[128,128]{1,0:T(8,128)}) custom-call(s32[1]{0:T(128)} %bitcast.refs_0_.at_ref, f32[4,48,128]{2,1,0:T(8,128)S(1)} %all_to_all.28.parts_ref), custom_call_target="tpu_custom_call" | custom-call | tf_op jit(solution)/shard_map/forcing/pallas_call | solution.py:416
  52.1 7.1 %all-to-all-start.2 = ((f32[128,1,128]{2,1,0:T(1,128)}), f32[128,1,128]{2,1,0:T(1,128)S(1)}, u32[]{:S(2)}, u32[]{:S(2)}) async-start(f32[128,1,128]{2,1,0:T(1,128)} %bitcast.11), calls=%async_computation.2 | async-start | bytes 131072 | tf_op jit(solution)/shard_map/all_to_all | solution.py:424
  59.2 6.6 %update.1 = f32[5184,128]{1,0:T(8,128)} custom-call(s32[1]{0:T(128)} %bitcast.refs_0_.at_ref, f32[4,18]{1,0:T(4,128)S(1)} %copy-done.1, f32[5184,128]{1,0:T(8,128)} %get-tuple-element.17.refs_2_, f32[72,128]{1,0:T(8,128)S(1)} %get-tuple-element.18.refs_2_.refs_3_, f32[16,128]{1,0:T(8,128)S(1)} %get-tuple-element.23.refs_4_, ...), custom_call_target="tpu_custom_call" | custom-call | flops 1990656 | bytes 5308416 | tf_op jit(solution)/shard_map/update/pallas_call | solution.py:425
  65.8 5.0 %all-to-all-done.2 = f32[128,1,128]{2,1,0:T(1,128)S(1)} async-done(((f32[128,1,128]{2,1,0:T(1,128)}), f32[128,1,128]{2,1,0:T(1,128)S(1)}, u32[]{:S(2)}, u32[]{:S(2)}) %all-to-all-start.2) | async-done | bytes 65568 | tf_op jit(solution)/shard_map/all_to_all | solution.py:424
  70.8 0.7 rows.1
Async XLA Ops:
  0.6 36.5 %copy-start.1 = (f32[4,18]{1,0:T(4,128)S(1)}, f32[4,18]{1,0:T(4,128)}, u32[]{:S(2)}) copy-start(f32[4,18]{1,0:T(4,128)} %constant.15.clone.refs_1_) | copy-start | bytes 868
  0.6 36.5 %copy-start = (s32[16,128]{1,0:T(8,128)S(1)}, s32[16,128]{1,0:T(8,128)}, u32[]{:S(2)}) copy-start(s32[16,128]{1,0:T(8,128)} %refs_5_.1) | copy-start | bytes 24580
  2.8 39.2 %collective-permute-start = (f32[368,128]{1,0:T(8,128)S(1)}, f32[368,128]{1,0:T(8,128)S(1)}, u32[]{:S(2)}, u32[]{:S(2)}) collective-permute-start(f32[368,128]{1,0:T(8,128)S(1)} %get-tuple-element.19.refs_5_), channel_id=1, source_target_pairs={{0,4},{8,12},{16,20},{24,28},{32,36},{40,44},{48,52},{56,60},{64,6... | collective-permute-start | bytes 565256 | tf_op jit(solution)/shard_map/ppermute | solution.py:386
  11.5 30.4 %collective-permute-start.1 = (f32[368,128]{1,0:T(8,128)S(1)}, f32[368,128]{1,0:T(8,128)S(1)}, u32[]{:S(2)}, u32[]{:S(2)}) collective-permute-start(f32[368,128]{1,0:T(8,128)S(1)} %get-tuple-element.20.refs_6_), channel_id=1, source_target_pairs={{4,8},{12,16},{20,24},{28,32},{36,40},{44,48},{52,56},{60,64},{68,... | collective-permute-start | bytes 565256 | tf_op jit(solution)/shard_map/ppermute | solution.py:385
  52.1 18.7 %all-to-all-start.2 = ((f32[128,1,128]{2,1,0:T(1,128)}), f32[128,1,128]{2,1,0:T(1,128)S(1)}, u32[]{:S(2)}, u32[]{:S(2)}) async-start(f32[128,1,128]{2,1,0:T(1,128)} %bitcast.11), calls=%async_computation.2 | async-start | bytes 131072 | tf_op jit(solution)/shard_map/all_to_all | solution.py:424

commit v5 on v4

--- a/solution.py
+++ b/solution.py
@@ -236,8 +236,8 @@
     at_ref,
     trig_ref,
     cell_ref,
-    from_pair_ref,
-    from_next_ref,
+    from_pair_hbm,
+    from_next_hbm,
     to_pair_ref,
     to_next_ref,
     parts_ref,
@@ -245,12 +245,23 @@
     fix_ref,
     behind_ref,
     ahead_ref,
+    from_pair_ref,
+    from_next_ref,
+    sems,
 ):
     bins = dirs * freqs
+    copies = [
+        pltpu.make_async_copy(from_pair_hbm, from_pair_ref, sems.at[0]),
+        pltpu.make_async_copy(from_next_hbm, from_next_ref, sems.at[1]),
+    ]
+    for copy in copies:
+        copy.start()
     odd, at = at_ref[0] >= BANDS, at_ref[0] % BANDS
     power = lax.broadcasted_iota(jnp.int32, (freqs, LANES), 0).astype(jnp.float32) - (freqs - 1)
     weights = [jnp.exp(power * (p * math.log(RATIO_STEP))) for p in (2, 3, 4)]
     out_ref[...] = parts_ref[...]
+    for copy in copies:
+        copy.wait()
     faces = (
         (0, 1.0, from_pair_ref, from_next_ref, to_pair_ref, to_next_ref),
         (ROWS - 1, -1.0, to_next_ref, to_pair_ref, from_next_ref, from_pair_ref),
@@ -382,8 +393,8 @@
     pairs = [(i, i + 1) for i in range(0, blocks, 2)]
     nexts = [(i, i + 1) for i in range(1, blocks - 1, 2)]
     got = held(lax.all_to_all(messages, BLK, 0, 0, tiled=True))
-    from_next = held(lax.ppermute(to_next, BLK, nexts + [(j, i) for i, j in nexts]))
-    from_pair = held(lax.ppermute(to_pair, BLK, pairs + [(j, i) for i, j in pairs]))
+    from_next = far(lax.ppermute(to_next, BLK, nexts + [(j, i) for i, j in nexts]))
+    from_pair = far(lax.ppermute(to_pair, BLK, pairs + [(j, i) for i, j in pairs]))
     move = pl.pallas_call(
         lambda *refs: move_kernel(dirs, freqs, *refs),
         out_shape=(pltpu.HBM((bins * ROWS, LANES), jnp.float32), near(bands, 48, LANES), near(72, LANES)),
@@ -405,9 +416,9 @@
     parts, fixes = pl.pallas_call(
         lambda *refs: fix_kernel(dirs, freqs, *refs),
         out_shape=(near(bands, 48, LANES), near(2, bins, LANES)),
-        in_specs=[smem, smem] + vmem_specs(6),
+        in_specs=[smem, smem] + vmem_specs(1) + [pl.BlockSpec(memory_space=pltpu.HBM)] * 2 + vmem_specs(3),
         out_specs=tuple(vmem_specs(2)),
-        scratch_shapes=[VMEM((bins + freqs + 8, LANES), jnp.float32), VMEM((bins + freqs + 8, LANES), jnp.float32)],
+        scratch_shapes=[VMEM((bins + freqs + 8, LANES), jnp.float32)] * 4 + [pltpu.SemaphoreType.DMA((2,))],
         name="fix",
         compiler_params=pltpu.CompilerParams(vmem_limit_bytes=4 * MIB),
     )(at, trig, cell, from_pair, from_next, to_pair, to_next, parts)

time: 72 us -> 73.6 us (1.022)
  Pallas kernels: 15.8 us -> 16.8 us
    pallas_call x1, Pallas kernels: 0.93 us -> 1.93 us  [one_step(): pl.pallas_call(lambda *refs: fix_kernel(dirs, freqs, *refs), out_shape=(n...]
where the time goes in v5:
time: 73.6 us; the launch traced here: 73.1 us
  blocking collectives  32.1 us (44%)
  starting transfers between devices  17.7 us (24%)
  Pallas kernels  16.8 us (23%)
  waiting for transfers between devices  4.99 us (7%)
  between operations  0.74 us (1%)
    all_to_all x1, blocking collectives, one_step(): got = held(lax.all_to_all(messages, BLK, 0, 0, tiled=True))  23.7 us
    ppermute x1, starting transfers between devices, one_step(): lax.ppermute(to_pair, BLK, pairs + [(j, i) for i, j in pairs])  8.75 us
    all_to_all x1, blocking collectives, one_step(): parts = held(lax.all_to_all(parts, DIR, 0, 0, tiled=True))  8.47 us
    all_to_all x1, starting transfers between devices, one_step(): ocean = held(lax.all_to_all(own, BLK, 0, 0, tiled=True))  7.05 us
    pallas_call x1, Pallas kernels, one_step(): pl.pallas_call(lambda *refs: update_kernel(dirs, freqs, *refs), out_shape...  6.57 us
    all_to_all x1, waiting for transfers between devices, one_step(): ocean = held(lax.all_to_all(own, BLK, 0, 0, tiled=True))  4.98 us
    pallas_call x1, Pallas kernels, one_step(): moved, parts, cell = move(at, trig, got, flat, speed, route_slot)  4.8 us
    pallas_call x1, Pallas kernels, one_step(): pl.pallas_call(lambda *refs: outgoing_kernel(bins, freqs, *refs), out_sha...  2.09 us
  transfers between devices with their start and end apart: 3, of which 1 were waited for; matrix products, arithmetic and copies ran while one was open for 0% of the time, Pallas kernels for 16%

profile of v5, /device:TPU:1, one launch (start us, length us, event | category | flops | bytes accessed | tf_op | source)
XLA Modules:
  0.0 73.1 jit_solution(8222820701593837693)
XLA Ops:
  0.6 0.0 copy-start.1
  0.6 0.0 copy-start
  0.7 2.1 %outgoing.1 = (f32[128,128]{1,0:T(8,128)}, f32[368,128]{1,0:T(8,128)S(1)}, f32[368,128]{1,0:T(8,128)S(1)}, f32[5184,128]{1,0:T(8,128)S(1)}, f32[576,128]{1,0:T(8,128)S(1)}) custom-call(s32[1]{0:T(128)} %bitcast.refs_0_.at_ref, f32[2,16,128]{2,1,0:T(8,128)} %bitcast.22, f32[2,2048]{1,0:T(2,128)} %bitcast.23, f32[16,128]{1,0:T(8,128)} %bitcast.24, ...), custom_call_target="tpu_custom_call" | custom-call | tf_op jit(solution)/shard_map/outgoing/pallas_call | solution.py:362
  2.8 8.7 %collective-permute-start = (f32[368,128]{1,0:T(8,128)S(1)}, f32[368,128]{1,0:T(8,128)S(1)}, u32[]{:S(2)}, u32[]{:S(2)}) collective-permute-start(f32[368,128]{1,0:T(8,128)S(1)} %get-tuple-element.19.refs_5_), channel_id=1, source_target_pairs={{0,4},{8,12},{16,20},{24,28},{32,36},{40,44},{48,52},{56,60},{64,6... | collective-permute-start | bytes 565256 | tf_op jit(solution)/shard_map/ppermute | solution.py:397
  11.5 1.9 %collective-permute-start.1 = (f32[368,128]{1,0:T(8,128)S(1)}, f32[368,128]{1,0:T(8,128)S(1)}, u32[]{:S(2)}, u32[]{:S(2)}) collective-permute-start(f32[368,128]{1,0:T(8,128)S(1)} %get-tuple-element.20.refs_6_), channel_id=1, source_target_pairs={{4,8},{12,16},{20,24},{28,32},{36,40},{44,48},{52,56},{60,64},{68,... | collective-permute-start | bytes 565256 | tf_op jit(solution)/shard_map/ppermute | solution.py:396
  13.4 23.7 %all_to_all.27 = f32[128,1,128]{2,1,0:T(1,128)S(1)} all-to-all(f32[128,1,128]{2,1,0:T(1,128)} %bitcast.21), channel_id=1, replica_groups=mesh['blk'=128,'dir'=4] {'blk'}, dimensions={0} | all-to-all | bytes 131072 | tf_op jit(solution)/shard_map/all_to_all | solution.py:395
  37.1 0.0 copy-done.1
  37.1 0.0 copy-done
  37.1 4.8 %move.1 = (f32[5184,128]{1,0:T(8,128)}, f32[4,48,128]{2,1,0:T(8,128)S(1)}, f32[72,128]{1,0:T(8,128)S(1)}) custom-call(s32[1]{0:T(128)} %bitcast.refs_0_.at_ref, f32[4,18]{1,0:T(4,128)S(1)} %copy-done.1, f32[128,128]{1,0:T(8,128)S(1)} %bitcast.16, f32[5184,128]{1,0:T(8,128)S(1)} %get-tuple-element.15.refs_3_, f32[576,128]{1,0:T(8,128)S(1)} %get-tuple-element.16.refs_4_, ...), custom_call_target="tpu_custom_call" | custom-call | tf_op jit(solution)/shard_map/move/pallas_call | solution.py:415
  41.9 0.0 collective-permute-done.refs_3_
  41.9 0.0 copy-start.2
  41.9 0.0 collective-permute-done.1.refs_4_
  41.9 0.0 copy-start.3
  42.0 0.6 copy-done.2
  42.6 0.1 copy-done.3
  42.7 1.9 %fix.1 = (f32[4,48,128]{2,1,0:T(8,128)S(1)}, f32[2,324,128]{2,1,0:T(8,128)S(1)}) custom-call(s32[1]{0:T(128)} %bitcast.refs_0_.at_ref, f32[4,18]{1,0:T(4,128)S(1)} %copy-done.1, f32[72,128]{1,0:T(8,128)S(1)} %get-tuple-element.18.refs_2_.refs_3_, f32[368,128]{1,0:T(8,128)} %copy-done.2, f32[368,128]{1,0:T(8,128)} %copy-done.3, ...), custom_call_target="tpu_custom_call" | custom-call | tf_op jit(solution)/shard_map/fix/pallas_call | solution.py:416
  44.6 8.5 %all_to_all.28.parts_ref = f32[4,48,128]{2,1,0:T(8,128)S(1)} all-to-all(f32[4,48,128]{2,1,0:T(8,128)S(1)} %get-tuple-element.22), channel_id=1, replica_groups=mesh['blk'=128,'dir'=4] {'dir'}, dimensions={0} | all-to-all | bytes 196608 | tf_op jit(solution)/shard_map/all_to_all | solution.py:426
  53.1 0.7 %forcing.1 = (f32[16,128]{1,0:T(8,128)S(1)}, f32[128,128]{1,0:T(8,128)}) custom-call(s32[1]{0:T(128)} %bitcast.refs_0_.at_ref, f32[4,48,128]{2,1,0:T(8,128)S(1)} %all_to_all.28.parts_ref), custom_call_target="tpu_custom_call" | custom-call | tf_op jit(solution)/shard_map/forcing/pallas_call | solution.py:427
  53.8 7.0 %all-to-all-start.2 = ((f32[128,1,128]{2,1,0:T(1,128)}), f32[128,1,128]{2,1,0:T(1,128)S(1)}, u32[]{:S(2)}, u32[]{:S(2)}) async-start(f32[128,1,128]{2,1,0:T(1,128)} %bitcast.11), calls=%async_computation.2 | async-start | bytes 131072 | tf_op jit(solution)/shard_map/all_to_all | solution.py:435
  60.9 6.6 %update.1 = f32[5184,128]{1,0:T(8,128)} custom-call(s32[1]{0:T(128)} %bitcast.refs_0_.at_ref, f32[4,18]{1,0:T(4,128)S(1)} %copy-done.1, f32[5184,128]{1,0:T(8,128)} %get-tuple-element.17.refs_2_, f32[72,128]{1,0:T(8,128)S(1)} %get-tuple-element.18.refs_2_.refs_3_, f32[16,128]{1,0:T(8,128)S(1)} %get-tuple-element.23.refs_4_, ...), custom_call_target="tpu_custom_call" | custom-call | flops 1990656 | bytes 5308416 | tf_op jit(solution)/shard_map/update/pallas_call | solution.py:436
  67.4 5.0 %all-to-all-done.2 = f32[128,1,128]{2,1,0:T(1,128)S(1)} async-done(((f32[128,1,128]{2,1,0:T(1,128)}), f32[128,1,128]{2,1,0:T(1,128)S(1)}, u32[]{:S(2)}, u32[]{:S(2)}) %all-to-all-start.2) | async-done | bytes 65568 | tf_op jit(solution)/shard_map/all_to_all | solution.py:435
  72.4 0.7 rows.1
Async XLA Ops:
  0.6 36.5 %copy-start.1 = (f32[4,18]{1,0:T(4,128)S(1)}, f32[4,18]{1,0:T(4,128)}, u32[]{:S(2)}) copy-start(f32[4,18]{1,0:T(4,128)} %constant.15.clone.refs_1_) | copy-start | bytes 868
  0.6 36.5 %copy-start = (s32[16,128]{1,0:T(8,128)S(1)}, s32[16,128]{1,0:T(8,128)}, u32[]{:S(2)}) copy-start(s32[16,128]{1,0:T(8,128)} %refs_5_.1) | copy-start | bytes 24580
  2.8 39.2 %collective-permute-start = (f32[368,128]{1,0:T(8,128)S(1)}, f32[368,128]{1,0:T(8,128)S(1)}, u32[]{:S(2)}, u32[]{:S(2)}) collective-permute-start(f32[368,128]{1,0:T(8,128)S(1)} %get-tuple-element.19.refs_5_), channel_id=1, source_target_pairs={{0,4},{8,12},{16,20},{24,28},{32,36},{40,44},{48,52},{56,60},{64,6... | collective-permute-start | bytes 565256 | tf_op jit(solution)/shard_map/ppermute | solution.py:397
  11.5 30.4 %collective-permute-start.1 = (f32[368,128]{1,0:T(8,128)S(1)}, f32[368,128]{1,0:T(8,128)S(1)}, u32[]{:S(2)}, u32[]{:S(2)}) collective-permute-start(f32[368,128]{1,0:T(8,128)S(1)} %get-tuple-element.20.refs_6_), channel_id=1, source_target_pairs={{4,8},{12,16},{20,24},{28,32},{36,40},{44,48},{52,56},{60,64},{68,... | collective-permute-start | bytes 565256 | tf_op jit(solution)/shard_map/ppermute | solution.py:396
  41.9 0.7 copy-start.2
  41.9 0.7 copy-start.3
  53.8 18.6 %all-to-all-start.2 = ((f32[128,1,128]{2,1,0:T(1,128)}), f32[128,1,128]{2,1,0:T(1,128)S(1)}, u32[]{:S(2)}, u32[]{:S(2)}) async-start(f32[128,1,128]{2,1,0:T(1,128)} %bitcast.11), calls=%async_computation.2 | async-start | bytes 131072 | tf_op jit(solution)/shard_map/all_to_all | solution.py:435

commit v6 on v4

--- a/solution.py
+++ b/solution.py
@@ -61,8 +61,11 @@
     out_ref,
     sems,
 ):
-    sources = (cur_hbm, wind_hbm, ice_hbm, slot_hbm, speed_hbm, spec_hbm)
-    targets = (cur_ref, wind_ref, ice_ref, slot_ref, speed_ref, spec_ref)
+    cut = bins // 24 * 8
+    starts = (0, cut, 2 * cut, bins)
+    parts = [pl.ds(a * ROWS, (b - a) * ROWS) for a, b in zip(starts, starts[1:])]
+    sources = (cur_hbm, wind_hbm, ice_hbm, slot_hbm, speed_hbm, *(spec_hbm.at[p, :] for p in parts))
+    targets = (cur_ref, wind_ref, ice_ref, slot_ref, speed_ref, *(spec_ref.at[p, :] for p in parts))
     copies = [pltpu.make_async_copy(a, b, sems.at[i]) for i, (a, b) in enumerate(zip(sources, targets))]
     for copy in copies:
         copy.start()
@@ -91,18 +94,23 @@
     sending = pltpu.make_async_copy(out_ref, sent_hbm, sems.at[len(sources)])
     sending.start()
     odd = at_ref[0] >= BANDS
-    for copy in copies[3:]:
-        copy.wait()
 
     def trade(start, stop, first, last):
         pair_ref[start:stop, :] = jnp.where(odd, first, last)
         next_ref[start:stop, :] = jnp.where(odd, last, first)
 
-    for source, start, count in ((spec_ref, 0, bins), (speed_ref, bins, freqs)):
-        trade(start, start + count, source[pl.ds(0, count, stride=ROWS), :], source[pl.ds(ROWS - 1, count, stride=ROWS), :])
+    def rows_of(source, start, count, row):
+        return source[pl.ds(start * ROWS + row, count, stride=ROWS), :]
+
+    copies[3].wait()
     sea = jnp.where(slot_ref[...] >= 0, 1.0, 0.0)
     sea = [jnp.broadcast_to(sea[r : r + 1, :], (8, LANES)) for r in (0, ROWS - 1)]
     trade(bins + freqs, bins + freqs + 8, *sea)
+    copies[4].wait()
+    trade(bins, bins + freqs, *(rows_of(speed_ref, 0, freqs, r) for r in (0, ROWS - 1)))
+    for copy, start, stop in zip(copies[5:], starts, starts[1:]):
+        copy.wait()
+        trade(start, stop, *(rows_of(spec_ref, start, stop - start, r) for r in (0, ROWS - 1)))
     sending.wait()
 
 
@@ -366,7 +374,7 @@
             VMEM((ROWS, LANES), jnp.int32),
             VMEM((2, ROWS, LANES), jnp.float32),
             VMEM((LANES, LANES), jnp.float32),
-            pltpu.SemaphoreType.DMA((7,)),
+            pltpu.SemaphoreType.DMA((9,)),
         ],
         name="outgoing",
         compiler_params=pltpu.CompilerParams(vmem_limit_bytes=8 * MIB),

time: 72 us -> 71.8 us (level)
  no operation moved by 1% of the time
where the time goes in v6:
time: 71.8 us; the launch traced here: 71.4 us
  blocking collectives  32.1 us (45%)
  starting transfers between devices  17.8 us (25%)
  Pallas kernels  15.7 us (22%)
  waiting for transfers between devices  5.04 us (7%)
  between operations  0.72 us (1%)
    all_to_all x1, blocking collectives, one_step(): got = held(lax.all_to_all(messages, BLK, 0, 0, tiled=True))  23.7 us
    ppermute x1, starting transfers between devices, one_step(): lax.ppermute(to_pair, BLK, pairs + [(j, i) for i, j in pairs])  8.75 us
    all_to_all x1, blocking collectives, one_step(): parts = held(lax.all_to_all(parts, DIR, 0, 0, tiled=True))  8.47 us
    all_to_all x1, starting transfers between devices, one_step(): ocean = held(lax.all_to_all(own, BLK, 0, 0, tiled=True))  7.12 us
    pallas_call x1, Pallas kernels, one_step(): pl.pallas_call(lambda *refs: update_kernel(dirs, freqs, *refs), out_shape...  6.57 us
    all_to_all x1, waiting for transfers between devices, one_step(): ocean = held(lax.all_to_all(own, BLK, 0, 0, tiled=True))  5.04 us
    pallas_call x1, Pallas kernels, one_step(): moved, parts, cell = move(at, trig, got, flat, speed, route_slot)  4.81 us
    pallas_call x1, Pallas kernels, one_step(): pl.pallas_call(lambda *refs: outgoing_kernel(bins, freqs, *refs), out_sha...  1.98 us
  transfers between devices with their start and end apart: 3, of which 1 were waited for; matrix products, arithmetic and copies ran while one was open for 0% of the time, Pallas kernels for 16%

profile of v6, /device:TPU:1, one launch (start us, length us, event | category | flops | bytes accessed | tf_op | source)
XLA Modules:
  0.0 71.4 jit_solution(3965928427255352655)
XLA Ops:
  0.6 0.0 copy-start.1
  0.6 0.0 copy-start
  0.7 2.0 %outgoing.1 = (f32[128,128]{1,0:T(8,128)}, f32[368,128]{1,0:T(8,128)S(1)}, f32[368,128]{1,0:T(8,128)S(1)}, f32[5184,128]{1,0:T(8,128)S(1)}, f32[576,128]{1,0:T(8,128)S(1)}) custom-call(s32[1]{0:T(128)} %bitcast.refs_0_.at_ref, f32[2,16,128]{2,1,0:T(8,128)} %bitcast.22, f32[2,2048]{1,0:T(2,128)} %bitcast.23, f32[16,128]{1,0:T(8,128)} %bitcast.24, ...), custom_call_target="tpu_custom_call" | custom-call | tf_op jit(solution)/shard_map/outgoing/pallas_call | solution.py:359
  2.6 8.7 %collective-permute-start = (f32[368,128]{1,0:T(8,128)S(1)}, f32[368,128]{1,0:T(8,128)S(1)}, u32[]{:S(2)}, u32[]{:S(2)}) collective-permute-start(f32[368,128]{1,0:T(8,128)S(1)} %get-tuple-element.19.refs_5_), channel_id=1, source_target_pairs={{0,4},{8,12},{16,20},{24,28},{32,36},{40,44},{48,52},{56,60},{64,6... | collective-permute-start | bytes 565256 | tf_op jit(solution)/shard_map/ppermute | solution.py:394
  11.4 1.9 %collective-permute-start.1 = (f32[368,128]{1,0:T(8,128)S(1)}, f32[368,128]{1,0:T(8,128)S(1)}, u32[]{:S(2)}, u32[]{:S(2)}) collective-permute-start(f32[368,128]{1,0:T(8,128)S(1)} %get-tuple-element.20.refs_6_), channel_id=1, source_target_pairs={{4,8},{12,16},{20,24},{28,32},{36,40},{44,48},{52,56},{60,64},{68,... | collective-permute-start | bytes 565256 | tf_op jit(solution)/shard_map/ppermute | solution.py:393
  13.3 23.7 %all_to_all.27 = f32[128,1,128]{2,1,0:T(1,128)S(1)} all-to-all(f32[128,1,128]{2,1,0:T(1,128)} %bitcast.21), channel_id=1, replica_groups=mesh['blk'=128,'dir'=4] {'blk'}, dimensions={0} | all-to-all | bytes 131072 | tf_op jit(solution)/shard_map/all_to_all | solution.py:392
  37.0 0.0 copy-done.1
  37.0 0.0 copy-done
  37.0 4.8 %move.1 = (f32[5184,128]{1,0:T(8,128)}, f32[4,48,128]{2,1,0:T(8,128)S(1)}, f32[72,128]{1,0:T(8,128)S(1)}) custom-call(s32[1]{0:T(128)} %bitcast.refs_0_.at_ref, f32[4,18]{1,0:T(4,128)S(1)} %copy-done.1, f32[128,128]{1,0:T(8,128)S(1)} %bitcast.16, f32[5184,128]{1,0:T(8,128)S(1)} %get-tuple-element.15.refs_3_, f32[576,128]{1,0:T(8,128)S(1)} %get-tuple-element.16.refs_4_, ...), custom_call_target="tpu_custom_call" | custom-call | tf_op jit(solution)/shard_map/move/pallas_call | solution.py:412
  41.8 0.0 collective-permute-done.refs_3_
  41.8 0.0 collective-permute-done.1.refs_4_
  41.8 0.9 %fix.1 = (f32[4,48,128]{2,1,0:T(8,128)S(1)}, f32[2,324,128]{2,1,0:T(8,128)S(1)}) custom-call(s32[1]{0:T(128)} %bitcast.refs_0_.at_ref, f32[4,18]{1,0:T(4,128)S(1)} %copy-done.1, f32[72,128]{1,0:T(8,128)S(1)} %get-tuple-element.18.refs_2_.refs_3_, f32[368,128]{1,0:T(8,128)S(1)} %collective-permute-done.refs_3_, ...), custom_call_target="tpu_custom_call" | custom-call | tf_op jit(solution)/shard_map/fix/pallas_call | solution.py:413
  42.8 8.5 %all_to_all.28.parts_ref = f32[4,48,128]{2,1,0:T(8,128)S(1)} all-to-all(f32[4,48,128]{2,1,0:T(8,128)S(1)} %get-tuple-element.22), channel_id=1, replica_groups=mesh['blk'=128,'dir'=4] {'dir'}, dimensions={0} | all-to-all | bytes 196608 | tf_op jit(solution)/shard_map/all_to_all | solution.py:423
  51.2 0.7 %forcing.1 = (f32[16,128]{1,0:T(8,128)S(1)}, f32[128,128]{1,0:T(8,128)}) custom-call(s32[1]{0:T(128)} %bitcast.refs_0_.at_ref, f32[4,48,128]{2,1,0:T(8,128)S(1)} %all_to_all.28.parts_ref), custom_call_target="tpu_custom_call" | custom-call | tf_op jit(solution)/shard_map/forcing/pallas_call | solution.py:424
  52.0 7.1 %all-to-all-start.2 = ((f32[128,1,128]{2,1,0:T(1,128)}), f32[128,1,128]{2,1,0:T(1,128)S(1)}, u32[]{:S(2)}, u32[]{:S(2)}) async-start(f32[128,1,128]{2,1,0:T(1,128)} %bitcast.11), calls=%async_computation.2 | async-start | bytes 131072 | tf_op jit(solution)/shard_map/all_to_all | solution.py:432
  59.1 6.6 %update.1 = f32[5184,128]{1,0:T(8,128)} custom-call(s32[1]{0:T(128)} %bitcast.refs_0_.at_ref, f32[4,18]{1,0:T(4,128)S(1)} %copy-done.1, f32[5184,128]{1,0:T(8,128)} %get-tuple-element.17.refs_2_, f32[72,128]{1,0:T(8,128)S(1)} %get-tuple-element.18.refs_2_.refs_3_, f32[16,128]{1,0:T(8,128)S(1)} %get-tuple-element.23.refs_4_, ...), custom_call_target="tpu_custom_call" | custom-call | flops 1990656 | bytes 5308416 | tf_op jit(solution)/shard_map/update/pallas_call | solution.py:433
  65.7 5.0 %all-to-all-done.2 = f32[128,1,128]{2,1,0:T(1,128)S(1)} async-done(((f32[128,1,128]{2,1,0:T(1,128)}), f32[128,1,128]{2,1,0:T(1,128)S(1)}, u32[]{:S(2)}, u32[]{:S(2)}) %all-to-all-start.2) | async-done | bytes 65568 | tf_op jit(solution)/shard_map/all_to_all | solution.py:432
  70.7 0.7 rows.1
Async XLA Ops:
  0.6 36.4 %copy-start.1 = (f32[4,18]{1,0:T(4,128)S(1)}, f32[4,18]{1,0:T(4,128)}, u32[]{:S(2)}) copy-start(f32[4,18]{1,0:T(4,128)} %constant.15.clone.refs_1_) | copy-start | bytes 868
  0.6 36.4 %copy-start = (s32[16,128]{1,0:T(8,128)S(1)}, s32[16,128]{1,0:T(8,128)}, u32[]{:S(2)}) copy-start(s32[16,128]{1,0:T(8,128)} %refs_5_.1) | copy-start | bytes 24580
  2.6 39.2 %collective-permute-start = (f32[368,128]{1,0:T(8,128)S(1)}, f32[368,128]{1,0:T(8,128)S(1)}, u32[]{:S(2)}, u32[]{:S(2)}) collective-permute-start(f32[368,128]{1,0:T(8,128)S(1)} %get-tuple-element.19.refs_5_), channel_id=1, source_target_pairs={{0,4},{8,12},{16,20},{24,28},{32,36},{40,44},{48,52},{56,60},{64,6... | collective-permute-start | bytes 565256 | tf_op jit(solution)/shard_map/ppermute | solution.py:394
  11.4 30.4 %collective-permute-start.1 = (f32[368,128]{1,0:T(8,128)S(1)}, f32[368,128]{1,0:T(8,128)S(1)}, u32[]{:S(2)}, u32[]{:S(2)}) collective-permute-start(f32[368,128]{1,0:T(8,128)S(1)} %get-tuple-element.20.refs_6_), channel_id=1, source_target_pairs={{4,8},{12,16},{20,24},{28,32},{36,40},{44,48},{52,56},{60,64},{68,... | collective-permute-start | bytes 565256 | tf_op jit(solution)/shard_map/ppermute | solution.py:393
  52.0 18.7 %all-to-all-start.2 = ((f32[128,1,128]{2,1,0:T(1,128)}), f32[128,1,128]{2,1,0:T(1,128)S(1)}, u32[]{:S(2)}, u32[]{:S(2)}) async-start(f32[128,1,128]{2,1,0:T(1,128)} %bitcast.11), calls=%async_computation.2 | async-start | bytes 131072 | tf_op jit(solution)/shard_map/all_to_all | solution.py:432
